TPU v7x, 32 devices: a whole 2x2x4 slice. The times are simulated.
32 devices in a mesh: dp: 8 (over z, x), expert: 4 (over y, core).
Axes of the slice: x: 2, y: 2, z: 4, core: 2. Of those that a mesh axis runs over, the one named last changes fastest.
Arguments:
- x_spans: bfloat16 [8, 8, 4, 16, 1536], P('dp', None, 'expert'), may hold values from -36 to 36
- crops: int32 [8, 4, 128, 1], P('dp', 'expert'), may hold values from 0 to 7; in each aligned block of 128 rows (0 to 127, 128 to 255, ..., all dimensions but the last counted through in order) at most 32 rows name the same one
- decay: float32 [8, 4, 128, 24], P('dp', 'expert'), may hold values from -1 to 0
- attn_gain: bfloat16 [1536], replicated, may hold values from 0.099609375 to 1.8984375
- w_query: bfloat16 [1536, 1536], replicated, may hold values from -0.15625 to 0.15625
- w_key: bfloat16 [1536, 1536], replicated, may hold values from -0.15625 to 0.15625
- w_value: bfloat16 [1536, 1536], replicated, may hold values from -0.15625 to 0.15625
- head_gain: bfloat16 [1536], replicated, may hold values from 0.099609375 to 1.8984375
- w_out: bfloat16 [1536, 1536], replicated, may hold values from -0.15625 to 0.15625
- moe_gain: bfloat16 [1536], replicated, may hold values from 0.099609375 to 1.8984375
- w_gate: bfloat16 [8, 1536, 6144], P('expert', None, 'dp'), may hold values from -0.15625 to 0.15625
- w_up: bfloat16 [8, 1536, 6144], P('expert', None, 'dp'), may hold values from -0.15625 to 0.15625
- w_down: bfloat16 [8, 6144, 1536], P('expert', 'dp'), may hold values from -0.078125 to 0.078125
Outputs:
- layer_out: bfloat16 [8, 4, 128, 1536], P('dp', 'expert')
Inputs may be any that keep to these rules, and one draw needn't show every extreme that they name: `crops`: within the tokens of one plot no crop is named more than 32 times, and some plot names some crop exactly 32 times.
All inputs are finite; a program needn't handle non-finite values.
Results may differ from a plain program's by a relative error of at most 0.012.
Values may be sent and summed in bfloat16 or wider, within the bound.
A program may use at most 128 MiB of HBM per device.

v0:
```python
import jax
import jax.numpy as jnp
from jax import lax
from jax.sharding import PartitionSpec as P

D = 1536
HEADS = 24
HEAD_DIM = 64
EXPERTS = 8
SPAN = 64


def rms_scale(values, width_eps):
    return lax.rsqrt(jnp.mean(values * values, axis=-1, keepdims=True) + width_eps)


def spread(buffers):
    return lax.all_gather(buffers, "dp", axis=0, tiled=True)


def deliver(buffers):
    return lax.all_to_all(buffers, "expert", split_axis=1, concat_axis=1, tiled=True)


def linear_mixing(query, key_vecs, value_vecs, forget, length):
    blocks = length // SPAN
    query_narrow = query.reshape(blocks, SPAN, HEADS, HEAD_DIM)
    key_narrow = key_vecs.reshape(blocks, SPAN, HEADS, HEAD_DIM)
    query_blocks = query_narrow.astype(jnp.float32)
    key_blocks = key_narrow.astype(jnp.float32)
    value_blocks = value_vecs.astype(jnp.float32).reshape(blocks, SPAN, HEADS, HEAD_DIM)
    within = jnp.cumsum(forget.reshape(blocks, SPAN, HEADS), axis=1)
    block_total = within[:, -1, :]
    scores = jnp.einsum(
        "nthd,nshd->nhts", query_narrow, key_narrow, preferred_element_type=jnp.float32
    )
    by_head = jnp.transpose(within, (0, 2, 1))
    spread_vals = by_head[:, :, :, None] - by_head[:, :, None, :]
    causal = jnp.arange(SPAN)[:, None] >= jnp.arange(SPAN)[None, :]
    weights = jnp.exp(jnp.where(causal[None, None], spread_vals, -jnp.inf))
    local_part = jnp.einsum(
        "nhts,nshd->nthd", scores * weights, value_blocks, precision=lax.Precision.HIGHEST
    )
    carried_keys = key_blocks * jnp.exp(block_total[:, None, :] - within)[..., None]
    block_states = jnp.einsum(
        "nshd,nshe->nhde", carried_keys, value_blocks, precision=lax.Precision.HIGHEST
    )

    def advance(carried, element):
        block_state, total_now = element
        return (carried * jnp.exp(total_now)[:, None, None] + block_state, carried)

    _, entering = lax.scan(
        advance, jnp.zeros((HEADS, HEAD_DIM, HEAD_DIM), jnp.float32), (block_states, block_total)
    )
    earlier_part = jnp.einsum(
        "nthd,nhde->nthe",
        query_blocks * jnp.exp(within)[..., None],
        entering,
        precision=lax.Precision.HIGHEST,
    )
    return (local_part + earlier_part).reshape(length, HEADS, HEAD_DIM)


def on_device(
    x_spans,
    crops,
    decay,
    attn_gain,
    w_query,
    w_key,
    w_value,
    head_gain,
    w_out,
    moe_gain,
    w_gate,
    w_up,
    w_down,
):
    arrived = lax.all_to_all(x_spans, "dp", split_axis=1, concat_axis=0, tiled=True)
    length = arrived.shape[0] * arrived.shape[3]
    tokens = arrived.reshape(length, D)
    forget = decay.reshape(length, HEADS)
    widened = tokens.astype(jnp.float32)
    normed = (widened * rms_scale(widened, 1e-05) * attn_gain.astype(jnp.float32)).astype(
        jnp.bfloat16
    )
    query = jnp.dot(normed, w_query, preferred_element_type=jnp.float32).astype(jnp.bfloat16)
    key_vecs = jnp.dot(normed, w_key, preferred_element_type=jnp.float32).astype(jnp.bfloat16)
    value_vecs = jnp.dot(normed, w_value, preferred_element_type=jnp.float32).astype(jnp.bfloat16)
    mixed = linear_mixing(query, key_vecs, value_vecs, forget, length)
    head_scale = head_gain.astype(jnp.float32).reshape(HEADS, HEAD_DIM)
    head_normed = (
        (mixed * rms_scale(mixed, 1e-05) * head_scale).reshape(length, D).astype(jnp.bfloat16)
    )
    resid = (widened + jnp.dot(head_normed, w_out, preferred_element_type=jnp.float32)).astype(
        jnp.bfloat16
    )
    resid_wide = resid.astype(jnp.float32)
    routed = (resid_wide * rms_scale(resid_wide, 1e-05) * moe_gain.astype(jnp.float32)).astype(
        jnp.bfloat16
    )
    crop_ids = crops.reshape(length)
    onehot = (crop_ids[:, None] == jnp.arange(EXPERTS, dtype=jnp.int32)[None, :]).astype(jnp.int32)
    slot_ids = jnp.sum((jnp.cumsum(onehot, axis=0) - onehot) * onehot, axis=1)
    capacity = length // 4
    position = crop_ids * capacity + slot_ids
    select = (jnp.arange(EXPERTS * capacity, dtype=jnp.int32)[:, None] == position[None, :]).astype(
        jnp.bfloat16
    )
    packed = jnp.dot(select, routed, preferred_element_type=jnp.float32).astype(jnp.bfloat16)
    owners = lax.axis_size("expert")
    local_count = w_gate.shape[0]
    outgoing = packed.reshape(1, owners, EXPERTS * capacity // owners, D)
    gathered = deliver(spread(outgoing))
    sources = gathered.shape[0]
    grouped = gathered.reshape(sources, owners, local_count, capacity, D)
    gate_act = jnp.einsum("sojcd,jdf->sojcf", grouped, w_gate, preferred_element_type=jnp.float32)
    up_act = jnp.einsum("sojcd,jdf->sojcf", grouped, w_up, preferred_element_type=jnp.float32)
    hidden = (jax.nn.silu(gate_act) * up_act).astype(jnp.bfloat16)
    term = jnp.einsum("sojcf,jfd->sojcd", hidden, w_down, preferred_element_type=jnp.float32)
    summed = lax.psum_scatter(
        term.reshape(1 * lax.axis_size("dp"), owners, local_count * capacity, D).astype(
            jnp.bfloat16
        ),
        "dp",
        scatter_dimension=0,
        tiled=True,
    )
    own_sums = summed[0]
    returned = lax.all_to_all(own_sums, "expert", split_axis=0, concat_axis=0, tiled=True)
    flat_back = returned.reshape(EXPERTS * capacity, D)
    expert_out = jnp.einsum("pl,pd->ld", select, flat_back, preferred_element_type=jnp.float32)
    layer_sum = (resid_wide + expert_out).astype(jnp.bfloat16)
    return layer_sum.reshape(1, 1, length, D)


def solution(mesh):
    return jax.shard_map(
        on_device,
        mesh=mesh,
        in_specs=(
            P("dp", None, "expert", None, None),
            P("dp", "expert", None, None),
            P("dp", "expert", None, None),
            P(),
            P(),
            P(),
            P(),
            P(),
            P(),
            P(),
            P("expert", None, "dp"),
            P("expert", None, "dp"),
            P("expert", "dp", None),
        ),
        out_specs=P("dp", "expert", None, None),
        check_vma=False,
    )
```

profile of v0, /device:TPU:0, one launch (start us, length us, event | category | flops | bytes accessed | tf_op | source)
XLA Modules:
  0.0 397.0 jit_solution(8698632406644414061)
XLA Ops:
  6.5 7.3 %all-to-all-start = ((bf16[1,8,1,16,1536]{4,3,2,0,1:T(8,128)(2,1)}), bf16[1,8,1,16,1536]{4,3,2,0,1:T(8,128)(2,1)S(1)}, u32[]{:S(2)}, u32[]{:S(2)}) async-start(bf16[1,8,1,16,1536]{4,3,2,0,1:T(8,128)(2,1)} %bitcast.97), calls=%async_computation | async-start | bytes 786432 | tf_op jit(solution)/shard_map/all_to_all | solution.py:80
  13.8 0.7 fusion.52
  16.7 0.8 copy.77
  20.4 0.8 select_reduce_fusion
  21.3 1.2 multiply_add_fusion
  22.5 3.0 all-to-all-done
  25.9 3.1 convolution_convert_fusion.1
  30.0 3.1 convolution_convert_fusion.2
  33.2 3.1 convolution_convert_fusion.3
  36.3 1.3 reshape.128
  38.1 0.9 copy-done
  39.0 1.5 fusion.45
  40.5 2.2 fusion.24
  42.7 3.8 while.13
  42.9 0.7 fusion.67
  43.6 1.0 bitcast_dynamic-update-slice_fusion.2
  45.4 0.9 bitcast_dynamic-update-slice_fusion.2
  46.5 3.6 fusion.27
  50.1 3.9 multiply_reduce_fusion
  54.2 1.2 copy.67
  56.3 3.5 multiply_reduce_fusion.1
  59.8 1.3 convolution_convert_fusion
  61.2 98.2 %all-gather.2.cloned.1.call-done = bf16[8,4,64,1536]{3,2,1,0:T(8,128)(2,1)} async-done(((bf16[1,4,64,1536]{3,2,1,0:T(8,128)(2,1)}), bf16[8,4,64,1536]{3,2,1,0:T(8,128)(2,1)}) %all-gather.2.cloned.1.call-update) | async-done | bytes 6291472 | tf_op jit(solution)/shard_map/all_gather | solution.py:18
  159.4 3.6 copy.68
  163.1 73.6 %all_to_all.19 = bf16[8,4,64,1536]{3,2,0,1:T(8,128)(2,1)S(1)} all-to-all(bf16[8,4,64,1536]{3,2,0,1:T(8,128)(2,1)S(1)} %copy.68), channel_id=1, replica_groups=mesh['dp'=8,'expert'=4] {'expert'}, dimensions={1} | all-to-all | bytes 12582912 | tf_op jit(solution)/shard_map/all_to_all | solution.py:22
  236.6 5.0 %fusion.6 = f32[2,8,4,32,768]{4,3,2,1,0:T(8,128)S(1)} fusion(bf16[8,4,2,32,1536]{4,3,2,0,1:T(8,128)(2,1)S(1)} %bitcast.90, bf16[2,1536,768]{2,1,0:T(8,128)(2,1)S(1)} %bitcast.104), kind=kOutput, calls=%fused_computation.13 | convolution fusion | flops 4831838208 | bytes 17301504 | tf_op jit(solution)/shard_map/sojcd,jdf->sojcf/dot_general | solution.py:119
  241.7 5.9 %fusion.2 = bf16[8,4,2,32,768]{4,3,1,0,2:T(8,128)(2,1)S(1)} fusion(f32[2,8,4,32,768]{4,3,2,1,0:T(8,128)S(1)} %fusion.6, bf16[2,1536,768]{2,1,0:T(8,128)(2,1)S(1)} %bitcast.106, bf16[8,4,2,32,1536]{4,3,2,0,1:T(8,128)(2,1)S(1)} %bitcast.91), kind=kOutput, calls=%fused_computation.6 | convolution fusion | flops 4841275392 | bytes 20447232 | tf_op jit(solution)/shard_map/sojcd,jdf->sojcf/dot_general | solution.py:118
  247.6 7.6 %convert_bitcast_fusion = bf16[8,4,2,32,1536]{4,3,1,0,2:T(8,128)(2,1)S(1)} fusion(bf16[8,4,2,32,768]{4,3,1,0,2:T(8,128)(2,1)S(1)} %fusion.2, bf16[2,768,1536]{2,1,0:T(8,128)(2,1)} %param.27), kind=kOutput, calls=%fused_computation.12 | convolution fusion | flops 4834983936 | bytes 14155776 | tf_op jit(solution)/shard_map/sojcf,jfd->sojcd/dot_general | solution.py:121
  255.2 3.4 copy.72
  258.6 115.4 %reduce-scatter.2.cloned.1.call-done = bf16[1,4,64,1536]{3,2,1,0:T(8,128)(2,1)} async-done(((bf16[8,4,64,1536]{3,2,1,0:T(8,128)(2,1)}), bf16[1,4,64,1536]{3,2,1,0:T(8,128)(2,1)}) %reduce-scatter.2.cloned.1.call-update) | async-done | bytes 786448 | tf_op jit(solution)/shard_map/reduce_scatter | solution.py:122
  374.0 15.1 %all_to_all.20 = bf16[4,64,1536]{2,1,0:T(8,128)(2,1)S(1)} all-to-all(bf16[4,64,1536]{2,1,0:T(8,128)(2,1)} %bitcast.95), channel_id=1, replica_groups=mesh['dp'=8,'expert'=4] {'expert'}, dimensions={0} | all-to-all | bytes 1572864 | tf_op jit(solution)/shard_map/all_to_all | solution.py:131
  389.1 1.1 fusion.20
  (53 shorter events, 9.1 us)
Async XLA Ops:
  6.5 18.9 %all-to-all-start = ((bf16[1,8,1,16,1536]{4,3,2,0,1:T(8,128)(2,1)}), bf16[1,8,1,16,1536]{4,3,2,0,1:T(8,128)(2,1)S(1)}, u32[]{:S(2)}, u32[]{:S(2)}) async-start(bf16[1,8,1,16,1536]{4,3,2,0,1:T(8,128)(2,1)} %bitcast.97), calls=%async_computation | async-start | bytes 786432 | tf_op jit(solution)/shard_map/all_to_all | solution.py:80
  13.8 145.6 %all-gather.2.cloned.1.call-start = ((), (), s32[]{:S(2)}) async-start(), calls=%async_computation.4 | async-start | bytes 7077888 | tf_op jit(solution)/shard_map/all_gather | solution.py:18
  17.6 8.1 %copy-start.3 = (f32[2,1,24]{2,1,0:T(1,128)}, f32[2,1,24]{2,1,0:T(1,128)S(1)}, u32[]{:S(2)}) copy-start(f32[2,1,24]{2,1,0:T(1,128)S(1)} %slice.4) | copy-start | bytes 580
  38.1 0.9 copy-start
  42.7 7.5 %copy-start.1 = (bf16[2,64,24,64]{3,2,1,0:T(8,128)(2,1)S(1)}, bf16[2,64,24,64]{3,2,1,0:T(8,128)(2,1)}, u32[]{:S(2)}) copy-start(bf16[2,64,24,64]{3,2,1,0:T(8,128)(2,1)} %copy-done) | copy-start | bytes 1179652
  46.5 3.6 copy-start.2
  55.9 3.9 copy-start.4
  61.2 312.8 %reduce-scatter.2.cloned.1.call-start = ((), (), s32[]{:S(2)}) async-start(), calls=%async_computation.5 | async-start | bytes 7077888 | tf_op jit(solution)/shard_map/reduce_scatter | solution.py:122
  159.4 77.2 %slice-start = ((s8[4718592]{0:T(1024)(128)(4,1)}), s8[4194304]{0:T(1024)(128)(4,1)S(1)}, s32[]{:S(2)}) async-start(s8[4718592]{0:T(1024)(128)(4,1)} %bitcast.103), calls=%async_computation.6 | async-start | bytes 8388608
  163.0 73.6 %slice-start.1 = ((s8[4718592]{0:T(1024)(128)(4,1)}), s8[524288]{0:T(1024)(128)(4,1)S(1)}, s32[]{:S(2)}) async-start(s8[4718592]{0:T(1024)(128)(4,1)} %bitcast.103), calls=%async_computation.7 | async-start | bytes 1048576
  163.1 78.6 %slice-start.2 = ((s8[4718592]{0:T(1024)(128)(4,1)}), s8[4194304]{0:T(1024)(128)(4,1)S(1)}, s32[]{:S(2)}) async-start(s8[4718592]{0:T(1024)(128)(4,1)} %bitcast.105), calls=%async_computation.8 | async-start | bytes 8388608
  236.6 5.0 %slice-start.3 = ((s8[4718592]{0:T(1024)(128)(4,1)}), s8[524288]{0:T(1024)(128)(4,1)S(1)}, s32[]{:S(2)}) async-start(s8[4718592]{0:T(1024)(128)(4,1)} %bitcast.105), calls=%async_computation.9 | async-start | bytes 1048576
Sparse Core Ops, SparseCore 0:
  61.3 98.0 all-gather.1
  258.7 115.1 reduce-scatter.1
where the time goes:
time: 398 us; the launch traced here: 397 us
  waiting for transfers between devices  217 us (55%)
  blocking collectives  88.7 us (22%)
  matrix products  44.9 us (11%)
  local copies, waits for them, and re-layouts  17.3 us (4%)
  between operations  13.7 us (3%)
  other arithmetic  8.3 us (2%)
  starting transfers between devices  7.33 us (2%)
    reduce_scatter x1, waiting for transfers between devices, on_device(): lax.psum_scatter(term.reshape(1 * lax.axis_size('dp'), owners, local_coun...  115 us
    all_gather x1, waiting for transfers between devices, spread(): return lax.all_gather(buffers, 'dp', axis=0, tiled=True)  98.2 us
    all_to_all x1, blocking collectives, deliver(): lax.all_to_all(buffers, 'expert', split_axis=1, concat_axis=1, tiled=True)  73.6 us
    all_to_all x1, blocking collectives, on_device(): lax.all_to_all(own_sums, 'expert', split_axis=0, concat_axis=0, tiled=True)  15.1 us
  transfers between devices with their start and end apart: 3, of which 3 were waited for; matrix products, arithmetic and copies ran while one was open for 2% of the time, Pallas kernels for 0%

commit v1 on v0

--- a/solution.py
+++ b/solution.py
@@ -112,7 +112,7 @@
     owners = lax.axis_size("expert")
     local_count = w_gate.shape[0]
     outgoing = packed.reshape(1, owners, EXPERTS * capacity // owners, D)
-    gathered = deliver(spread(outgoing))
+    gathered = spread(deliver(outgoing))
     sources = gathered.shape[0]
     grouped = gathered.reshape(sources, owners, local_count, capacity, D)
     gate_act = jnp.einsum("sojcd,jdf->sojcf", grouped, w_gate, preferred_element_type=jnp.float32)

time: 398 us -> 338 us (0.85)
  blocking collectives: 88.7 us -> 29.9 us
    all_to_all x1, blocking collectives: 73.6 us -> 14.8 us  [deliver(): lax.all_to_all(buffers, 'expert', split_axis=1, concat_axis=1, tiled=True)]
  transfers between devices with their start and end apart: 3 -> 3, of which waited for: 3 -> 3; matrix products, arithmetic and copies ran while one was open for 2% -> 3% of each run, Pallas kernels for 0% -> 0%
where the time goes in v1:
time: 338 us; the launch traced here: 337 us
  waiting for transfers between devices  217 us (64%)
  matrix products  47.8 us (14%)
  blocking collectives  29.9 us (9%)
  between operations  13.7 us (4%)
  local copies, waits for them, and re-layouts  13.6 us (4%)
  other arithmetic  8.3 us (2%)
  starting transfers between devices  7.33 us (2%)
    reduce_scatter x1, waiting for transfers between devices, on_device(): lax.psum_scatter(term.reshape(1 * lax.axis_size('dp'), owners, local_coun...  116 us
    all_gather x1, waiting for transfers between devices, spread(): return lax.all_gather(buffers, 'dp', axis=0, tiled=True)  97.2 us
    all_to_all x1, blocking collectives, on_device(): lax.all_to_all(own_sums, 'expert', split_axis=0, concat_axis=0, tiled=True)  15.1 us
    all_to_all x1, blocking collectives, deliver(): lax.all_to_all(buffers, 'expert', split_axis=1, concat_axis=1, tiled=True)  14.8 us
    dot_general x1, matrix products, on_device(): jnp.einsum('sojcd,jdf->sojcf', grouped, w_up, preferred_element_type=jnp....  8.68 us
    dot_general x1, matrix products, on_device(): jnp.einsum('sojcd,jdf->sojcf', grouped, w_gate, preferred_element_type=jn...  8.37 us
    all_to_all x1, starting transfers between devices, on_device(): lax.all_to_all(x_spans, 'dp', split_axis=1, concat_axis=0, tiled=True)  7.25 us
  transfers between devices with their start and end apart: 3, of which 3 were waited for; matrix products, arithmetic and copies ran while one was open for 3% of the time, Pallas kernels for 0%

profile of v1, /device:TPU:0, one launch (start us, length us, event | category | flops | bytes accessed | tf_op | source)
XLA Modules:
  0.0 337.4 jit_solution(17913030399810466076)
XLA Ops:
  6.5 7.3 %all-to-all-start = ((bf16[1,8,1,16,1536]{4,3,2,0,1:T(8,128)(2,1)}), bf16[1,8,1,16,1536]{4,3,2,0,1:T(8,128)(2,1)S(1)}, u32[]{:S(2)}, u32[]{:S(2)}) async-start(bf16[1,8,1,16,1536]{4,3,2,0,1:T(8,128)(2,1)} %bitcast.97), calls=%async_computation | async-start | bytes 786432 | tf_op jit(solution)/shard_map/all_to_all | solution.py:80
  13.8 0.7 fusion.52
  14.6 0.7 convert_element_type.77
  15.3 0.7 convert_element_type.84
  16.7 0.8 copy.77
  20.4 0.8 select_reduce_fusion
  21.2 1.2 multiply_add_fusion
  22.5 3.0 all-to-all-done
  25.9 3.1 convolution_convert_fusion.1
  30.0 3.1 convolution_convert_fusion.2
  33.2 3.1 convolution_convert_fusion.3
  36.3 1.3 reshape.128
  38.1 0.9 copy-done
  39.0 1.5 fusion.45
  40.5 2.2 fusion.24
  42.6 3.8 %while.13 = (s32[]{:T(128)}, f32[24,64,64]{2,1,0:T(8,128)S(1)}, f32[2,24,64,64]{3,2,1,0:T(8,128)}, f32[2,24]{1,0:T(2,128)}, f32[2,24,64,64]{3,2,1,0:T(8,128)S(1)}, /*index=5*/s32[]{:T(128)}, s32[]{:T(128)}) while((s32[]{:T(128)}, f32[24,64,64]{2,1,0:T(8,128)S(1)}, f32[2,24,64,64]{3,2,1,0:T(8,128)}, f32[2,24]{1,0:T(2,128)}, ...), condition=%wide.region_3.4_spmd.clone, body=%wide.region_2.3_spmd.clone.sunk | while | flops 393219 | bytes 2359692 | solution.py:53
  42.8 0.7 fusion.67
  43.6 1.0 bitcast_dynamic-update-slice_fusion.2
  45.4 0.9 bitcast_dynamic-update-slice_fusion.2
  46.5 3.6 %fusion.27 = f32[2,24,64,64]{3,2,1,0:T(8,128)S(1)} fusion(f32[2,24,64,64]{3,2,1,0:T(8,128)} %fusion.45, f32[2,24,64]{2,1,0:T(8,128)} %copy.56, pred[64,64]{1,0:T(8,128)(4,1)} %iota_compare_fusion.4, bf16[2,64,24,64]{3,2,1,0:T(8,128)(2,1)} %reshape.128), kind=kOutput, calls=%fused_computation.38 | convolution fusion | flops 151584768 | bytes 1982464 | tf_op jit(solution)/shard_map/nhts,nshd->nthd/dot_general | solution.py:41
  50.1 3.9 %multiply_reduce_fusion = (f32[2,64,24]{1,2,0:T(8,128)S(1)}, f32[2,64,24,64]{1,3,2,0:T(8,128)S(1)}) fusion(f32[2,24,64,64]{3,2,1,0:T(8,128)S(1)} %fusion.27, f32[2,24,64,64]{3,2,1,0:T(8,128)S(1)} %copy-done.2, f32[2,64,24]{1,2,0:T(8,128)} %copy.63, bf16[2,64,24,64]{3,2,1,0:T(8,128)(2,1)S(1)} %copy-done.1), kind=kOutput, calls=%fused_computation.30 | convolution fusion | flops 151974912 | bytes 2777088 | tf_op jit(solution)/shard_map/nthd,nhde->nthe/dot_general | solution.py:56
  54.2 1.1 copy.67
  56.3 3.5 %multiply_reduce_fusion.1 = (f32[128]{0:T(128)S(1)}, f32[128,1536]{1,0:T(8,128)S(1)}) fusion(bf16[1536,1536]{1,0:T(8,128)(2,1)} %param.23, f32[128,1536]{1,0:T(8,128)S(1)} %reshape.131, f32[128,1536]{1,0:T(8,128)} %copy.67, f32[1536]{0:T(1024)S(1)} %convert_element_type.84, bf16[128,1536]{1,0:T(8,128)(2,1)S(1)} %bitcast.90), kind=kOutput, calls=%fused_computation.47 | convolution fusion | flops 605749120 | bytes 7477760 | tf_op jit(solution)/shard_map/dot_general | solution.py:96
  60.2 14.8 %all_to_all.19 = bf16[1,4,64,1536]{3,2,0,1:T(8,128)(2,1)} all-to-all(bf16[1,4,64,1536]{3,2,0,1:T(8,128)(2,1)S(1)} %bitcast.94), channel_id=1, replica_groups=mesh['dp'=8,'expert'=4] {'expert'}, dimensions={1} | all-to-all | bytes 1572864 | tf_op jit(solution)/shard_map/all_to_all | solution.py:22
  75.1 97.2 %all-gather.2.cloned.1.call-done = bf16[8,4,64,1536]{3,2,1,0:T(8,128)(2,1)} async-done(((bf16[1,4,64,1536]{3,2,1,0:T(8,128)(2,1)}), bf16[8,4,64,1536]{3,2,1,0:T(8,128)(2,1)}) %all-gather.2.cloned.1.call-update) | async-done | bytes 6291472 | tf_op jit(solution)/shard_map/all_gather | solution.py:18
  172.3 8.7 %fusion.6 = f32[2,8,4,32,768]{4,3,2,1,0:T(8,128)S(1)} fusion(bf16[8,4,2,32,1536]{4,3,2,1,0:T(8,128)(2,1)} %bitcast.103, bf16[2,1536,768]{2,1,0:T(8,128)(2,1)} %param.26), kind=kOutput, calls=%fused_computation.13 | convolution fusion | flops 4831838208 | bytes 17301504 | tf_op jit(solution)/shard_map/sojcd,jdf->sojcf/dot_general | solution.py:119
  181.0 8.4 %fusion.2 = bf16[8,4,2,32,768]{4,3,1,0,2:T(8,128)(2,1)S(1)} fusion(f32[2,8,4,32,768]{4,3,2,1,0:T(8,128)S(1)} %fusion.6, bf16[2,1536,768]{2,1,0:T(8,128)(2,1)} %param.25, bf16[8,4,2,32,1536]{4,3,2,1,0:T(8,128)(2,1)S(1)} %bitcast.104), kind=kOutput, calls=%fused_computation.6 | convolution fusion | flops 4841275392 | bytes 20447232 | tf_op jit(solution)/shard_map/sojcd,jdf->sojcf/dot_general | solution.py:118
  189.4 5.2 %convert_bitcast_fusion = bf16[8,4,2,32,1536]{4,3,1,0,2:T(8,128)(2,1)S(1)} fusion(bf16[8,4,2,32,768]{4,3,1,0,2:T(8,128)(2,1)S(1)} %fusion.2, bf16[2,768,1536]{2,1,0:T(8,128)(2,1)S(1)} %bitcast.106), kind=kOutput, calls=%fused_computation.12 | convolution fusion | flops 4834983936 | bytes 14155776 | tf_op jit(solution)/shard_map/sojcf,jfd->sojcd/dot_general | solution.py:121
  194.7 3.4 %copy.72 = bf16[8,4,2,32,1536]{4,3,2,1,0:T(8,128)(2,1)} copy(bf16[8,4,2,32,1536]{4,3,1,0,2:T(8,128)(2,1)S(1)} %convert_bitcast_fusion) | data formatting | bytes 12582912 | tf_op jit(solution)/shard_map/convert_element_type | solution.py:123
  198.1 116.3 %reduce-scatter.2.cloned.1.call-done = bf16[1,4,64,1536]{3,2,1,0:T(8,128)(2,1)} async-done(((bf16[8,4,64,1536]{3,2,1,0:T(8,128)(2,1)}), bf16[1,4,64,1536]{3,2,1,0:T(8,128)(2,1)}) %reduce-scatter.2.cloned.1.call-update) | async-done | bytes 786448 | tf_op jit(solution)/shard_map/reduce_scatter | solution.py:122
  314.4 15.1 %all_to_all.20 = bf16[4,64,1536]{2,1,0:T(8,128)(2,1)S(1)} all-to-all(bf16[4,64,1536]{2,1,0:T(8,128)(2,1)} %bitcast.95), channel_id=1, replica_groups=mesh['dp'=8,'expert'=4] {'expert'}, dimensions={0} | all-to-all | bytes 1572864 | tf_op jit(solution)/shard_map/all_to_all | solution.py:131
  329.5 1.1 fusion.20
  (49 shorter events, 8.1 us)
Async XLA Ops:
  6.5 18.9 %all-to-all-start = ((bf16[1,8,1,16,1536]{4,3,2,0,1:T(8,128)(2,1)}), bf16[1,8,1,16,1536]{4,3,2,0,1:T(8,128)(2,1)S(1)}, u32[]{:S(2)}, u32[]{:S(2)}) async-start(bf16[1,8,1,16,1536]{4,3,2,0,1:T(8,128)(2,1)} %bitcast.97), calls=%async_computation | async-start | bytes 786432 | tf_op jit(solution)/shard_map/all_to_all | solution.py:80
  13.8 158.5 %all-gather.2.cloned.1.call-start = ((), (), s32[]{:S(2)}) async-start(), calls=%async_computation.4 | async-start | bytes 7077888 | tf_op jit(solution)/shard_map/all_gather | solution.py:18
  17.6 8.1 %copy-start.3 = (f32[2,1,24]{2,1,0:T(1,128)}, f32[2,1,24]{2,1,0:T(1,128)S(1)}, u32[]{:S(2)}) copy-start(f32[2,1,24]{2,1,0:T(1,128)S(1)} %slice.4) | copy-start | bytes 580
  38.1 0.9 copy-start
  42.6 7.4 %copy-start.1 = (bf16[2,64,24,64]{3,2,1,0:T(8,128)(2,1)S(1)}, bf16[2,64,24,64]{3,2,1,0:T(8,128)(2,1)}, u32[]{:S(2)}) copy-start(bf16[2,64,24,64]{3,2,1,0:T(8,128)(2,1)} %copy-done) | copy-start | bytes 1179652
  46.5 3.6 %copy-start.2 = (f32[2,24,64,64]{3,2,1,0:T(8,128)S(1)}, f32[2,24,64,64]{3,2,1,0:T(8,128)}, u32[]{:S(2)}) copy-start(f32[2,24,64,64]{3,2,1,0:T(8,128)} %get-tuple-element.32) | copy-start | bytes 2359300
  55.9 3.9 %copy-start.4 = (s32[128]{0:T(128)S(1)}, s32[128]{0:T(128)}, u32[]{:S(2)}) copy-start(s32[128]{0:T(128)} %multiply_add_fusion) | copy-start | bytes 1540
  75.0 239.4 %reduce-scatter.2.cloned.1.call-start = ((), (), s32[]{:S(2)}) async-start(), calls=%async_computation.5 | async-start | bytes 7077888 | tf_op jit(solution)/shard_map/reduce_scatter | solution.py:122
  172.3 8.7 %copy-start.5 = (bf16[8,4,64,1536]{3,2,1,0:T(8,128)(2,1)S(1)}, bf16[8,4,64,1536]{3,2,1,0:T(8,128)(2,1)}, u32[]{:S(2)}) copy-start(bf16[8,4,64,1536]{3,2,1,0:T(8,128)(2,1)} %all-gather.2.cloned.1.call-done) | copy-start | bytes 18874372
  172.3 17.1 %slice-start = ((s8[4718592]{0:T(1024)(128)(4,1)}), s8[4194304]{0:T(1024)(128)(4,1)S(1)}, s32[]{:S(2)}) async-start(s8[4718592]{0:T(1024)(128)(4,1)} %bitcast.105), calls=%async_computation.6 | async-start | bytes 8388608
  181.0 8.4 %slice-start.1 = ((s8[4718592]{0:T(1024)(128)(4,1)}), s8[524288]{0:T(1024)(128)(4,1)S(1)}, s32[]{:S(2)}) async-start(s8[4718592]{0:T(1024)(128)(4,1)} %bitcast.105), calls=%async_computation.7 | async-start | bytes 1048576
Sparse Core Ops, SparseCore 0:
  75.2 97.1 all-gather.1
  198.2 116.1 reduce-scatter.1

commit v2 on v1

--- a/solution.py
+++ b/solution.py
@@ -1,6 +1,8 @@
 import jax
 import jax.numpy as jnp
 from jax import lax
+from jax.experimental import pallas as pl
+from jax.experimental.pallas import tpu as pltpu
 from jax.sharding import PartitionSpec as P
 
 D = 1536
@@ -8,6 +10,399 @@
 HEAD_DIM = 64
 EXPERTS = 8
 SPAN = 64
+NZ = 4
+NX = 2
+NY = 2
+NC = 2
+CHIPS = NZ * NX * NY
+Z_UP, Z_DOWN, BY_X, BY_Y, CORE = range(5)
+
+
+def place():
+    dp, expert = lax.axis_index("dp"), lax.axis_index("expert")
+    return dp // NX, dp % NX, expert // NC, expert % NC
+
+
+def device(z, x, y, c):
+    return (z * NX + x, y * NC + c)
+
+
+def plot_of(z, x, y, c):
+    return (z * NX + x) * (NY * NC) + y * NC + c
+
+
+def chip_of(z, x, y):
+    return (z * NX + x) * NY + y
+
+
+def partner(kind, z, x, y, c):
+    if kind == Z_UP:
+        return device(z + 1, x, y, c)
+    if kind == Z_DOWN:
+        return device(z - 1, x, y, c)
+    if kind == BY_X:
+        return device(z, 1 - x, y, c)
+    if kind == BY_Y:
+        return device(z, x, 1 - y, c)
+    return device(z, x, y, 1 - c)
+
+
+def only_if(condition, body):
+    if condition is None:
+        body()
+    else:
+        pl.when(condition)(body)
+
+
+def exists(kind, z):
+    return {Z_UP: z < NZ - 1, Z_DOWN: z > 0}.get(kind)
+
+
+def greet(z, x, y, c):
+    barrier = pltpu.get_barrier_semaphore()
+    for kind in range(5):
+
+        def signal(kind=kind):
+            pl.semaphore_signal(
+                barrier,
+                inc=1,
+                device_id=partner(kind, z, x, y, c),
+                device_id_type=pl.DeviceIdType.MESH,
+            )
+
+        only_if(exists(kind, z), signal)
+    pl.semaphore_wait(barrier, 3 + jnp.where(z > 0, 1, 0) + jnp.where(z < NZ - 1, 1, 0))
+
+
+def gather_kernel(own_ref, out_ref, send_sem, recv_sem, core_sem, local_sem):
+    z, x, y, c = place()
+    half = own_ref.shape[0] // 2
+    greet(z, x, y, c)
+    sent = []
+
+    def rows(h):
+        return pl.ds(h * half, half)
+
+    def copy(h, kind, bz, bx, by, own):
+        chip = chip_of(bz, bx, by)
+        target = out_ref.at[plot_of(bz, bx, by, c), rows(h)]
+        return pltpu.make_async_remote_copy(
+            src_ref=own_ref.at[rows(h)] if own else target,
+            dst_ref=target,
+            send_sem=send_sem.at[h, kind, chip],
+            recv_sem=(core_sem if kind == CORE else recv_sem).at[h, chip],
+            device_id=partner(kind, z, x, y, c),
+            device_id_type=pl.DeviceIdType.MESH,
+        )
+
+    def send(h, kind, bz, bx, by, guard, own=False):
+        def both(action):
+            def body():
+                def inner():
+                    action(copy(h, kind, bz, bx, by, own))
+
+                only_if(exists(kind, z), inner)
+
+            only_if(guard, body)
+
+        both(lambda made: made.start())
+        sent.append(lambda: both(lambda made: made.wait_send()))
+
+    def arrive(h, bz, bx, by, guard):
+        only_if(guard, lambda: copy(h, BY_X, bz, bx, by, False).wait_recv())
+
+    stay = pltpu.make_async_copy(own_ref, out_ref.at[plot_of(z, x, y, c)], local_sem)
+    stay.start()
+    middle = (BY_X, BY_Y)
+    last = (BY_Y, BY_X)
+    for h in range(2):
+        for kind in (Z_UP, Z_DOWN, middle[h], last[h], CORE):
+            send(h, kind, z, x, y, None, own=True)
+
+    def spots(step):
+        if step == 0:
+            return [(z, None, None)]
+        return [(z - step, z - step >= 0, Z_UP), (z + step, z + step < NZ, Z_DOWN)]
+
+    for turn in range(NZ + 2):
+        if 1 <= turn < NZ:
+            for bz, guard, way in spots(turn):
+                for h in range(2):
+                    arrive(h, bz, x, y, guard)
+                    for kind in (way, middle[h], last[h], CORE):
+                        send(h, kind, bz, x, y, guard)
+        if 0 <= turn - 1 < NZ:
+            for bz, guard, _ in spots(turn - 1):
+                for h in range(2):
+                    bx, by = (1 - x, y) if h == 0 else (x, 1 - y)
+                    arrive(h, bz, bx, by, guard)
+                    for kind in (last[h], CORE):
+                        send(h, kind, bz, bx, by, guard)
+        if 0 <= turn - 2 < NZ:
+            for bz, guard, _ in spots(turn - 2):
+                for h in range(2):
+                    for bx, by in ((x, 1 - y), (1 - x, 1 - y)) if h == 0 else ((1 - x, y), (1 - x, 1 - y)):
+                        arrive(h, bz, bx, by, guard)
+                        send(h, CORE, bz, bx, by, guard)
+    for chip in range(CHIPS):
+        bz, bx, by = chip // (NX * NY), chip // NY % NX, chip % NY
+        for h in range(2):
+            landed = out_ref.at[plot_of(bz, bx, by, 1 - c), rows(h)]
+            pltpu.make_async_remote_copy(
+                src_ref=landed,
+                dst_ref=landed,
+                send_sem=send_sem.at[h, CORE, chip],
+                recv_sem=core_sem.at[h, chip],
+                device_id=partner(CORE, z, x, y, c),
+                device_id_type=pl.DeviceIdType.MESH,
+            ).wait_recv()
+    for wait in sent:
+        wait()
+    stay.wait()
+
+
+def gather_plots(own):
+    length = own.shape[0]
+    plots = CHIPS * NC
+    return pl.pallas_call(
+        gather_kernel,
+        out_shape=jax.ShapeDtypeStruct((plots, length, D), jnp.bfloat16),
+        in_specs=[pl.BlockSpec(memory_space=pltpu.VMEM)],
+        out_specs=pl.BlockSpec(memory_space=pl.ANY),
+        scratch_shapes=[
+            pltpu.SemaphoreType.DMA((2, 5, CHIPS)),
+            pltpu.SemaphoreType.DMA((2, CHIPS)),
+            pltpu.SemaphoreType.DMA((2, CHIPS)),
+            pltpu.SemaphoreType.DMA,
+        ],
+        compiler_params=pltpu.CompilerParams(collective_id=0, has_side_effects=True),
+    )(own)
+
+
+def reduce_kernel(
+    terms_ref,
+    out_ref,
+    core_buf,
+    first_buf,
+    second_buf,
+    up_buf,
+    down_buf,
+    core_sem,
+    first_sem,
+    second_sem,
+    up_sem,
+    down_sem,
+):
+    z, x, y, c = place()
+    half = out_ref.shape[0] // 2
+    greet(z, x, y, c)
+    sent = []
+
+    def rows(h):
+        return pl.ds(h * half, half)
+
+    def move(src, buf, sem, index, kind):
+        return pltpu.make_async_remote_copy(
+            src_ref=src,
+            dst_ref=buf.at[index],
+            send_sem=sem.at[(0, *index)],
+            recv_sem=sem.at[(1, *index)],
+            device_id=partner(kind, z, x, y, c),
+            device_id_type=pl.DeviceIdType.MESH,
+        )
+
+    def send(src, buf, sem, index, kind, guard=None):
+        only_if(guard, lambda: move(src, buf, sem, index, kind).start())
+        sent.append(lambda: only_if(guard, lambda: move(src, buf, sem, index, kind).wait_send()))
+
+    def arrive(buf, sem, index, kind):
+        move(buf.at[index], buf, sem, index, kind).wait_recv()
+
+    def wide(ref, *index):
+        return ref[index].astype(jnp.float32)
+
+    low = jnp.where(z < NZ // 2, 1, 0)
+
+    def layer(turn):
+        return low * (NZ - 1 - turn) + (1 - low) * turn
+
+    def spot(h, first_other, second_other):
+        first, second = (y, x) if h == 0 else (x, y)
+        first = 1 - first if first_other else first
+        second = 1 - second if second_other else second
+        return (second, first) if h == 0 else (first, second)
+
+    order = ((1, 1), (1, 0), (0, 1), (0, 0))
+    first_kind, second_kind = (BY_Y, BY_X), (BY_X, BY_Y)
+    for turn in range(NZ):
+        for first_other, second_other in order:
+            for h in range(2):
+                bx, by = spot(h, first_other, second_other)
+                bz = layer(turn)
+                send(
+                    terms_ref.at[plot_of(bz, bx, by, 1 - c), rows(h)],
+                    core_buf,
+                    core_sem,
+                    (h, chip_of(bz, bx, by)),
+                    CORE,
+                )
+
+    def pair(turn):
+        bz = layer(turn)
+        for first_other, second_other in order:
+            for h in range(2):
+                bx, by = spot(h, first_other, second_other)
+                index = (h, chip_of(bz, bx, by))
+                arrive(core_buf, core_sem, index, CORE)
+                total = wide(core_buf, *index) + wide(
+                    terms_ref, plot_of(bz, bx, by, c), rows(h)
+                )
+                core_buf[index] = total.astype(jnp.bfloat16)
+                if first_other:
+                    second = bx if h == 0 else by
+                    send(
+                        core_buf.at[index], first_buf, first_sem, (h, bz, second), first_kind[h]
+                    )
+
+    def across(turn):
+        bz = layer(turn)
+        for h in range(2):
+            bx, by = spot(h, 0, 1)
+            index = (h, bz, bx if h == 0 else by)
+            arrive(first_buf, first_sem, index, first_kind[h])
+            total = wide(first_buf, *index) + wide(core_buf, h, chip_of(bz, bx, by))
+            first_buf[index] = total.astype(jnp.bfloat16)
+            send(first_buf.at[index], second_buf, second_sem, (h, bz), second_kind[h])
+
+    def along(turn):
+        bz = layer(turn)
+        for h in range(2):
+            bx, by = spot(h, 0, 0)
+            index = (h, bz, bx if h == 0 else by)
+            arrive(first_buf, first_sem, index, first_kind[h])
+            arrive(second_buf, second_sem, (h, bz), second_kind[h])
+            total = (
+                wide(first_buf, *index)
+                + wide(core_buf, h, chip_of(bz, bx, by))
+                + wide(second_buf, h, bz)
+            )
+            for buf, sem, kind, goes, comes in (
+                (up_buf, up_sem, Z_UP, bz > z, z > 0),
+                (down_buf, down_sem, Z_DOWN, bz < z, z < NZ - 1),
+            ):
+
+                @pl.when(goes)
+                def _():
+                    @pl.when(comes)
+                    def _():
+                        arrive(buf, sem, (h, bz), kind)
+                        buf[h, bz] = (total + wide(buf, h, bz)).astype(jnp.bfloat16)
+
+                    @pl.when(jnp.logical_not(comes))
+                    def _():
+                        buf[h, bz] = total.astype(jnp.bfloat16)
+
+                send(buf.at[h, bz], buf, sem, (h, bz), kind, goes)
+
+    for turn in range(NZ + 2):
+        if turn < NZ:
+            pair(turn)
+        if 0 <= turn - 1 < NZ:
+            across(turn - 1)
+        if 0 <= turn - 2 < NZ:
+            along(turn - 2)
+    for h in range(2):
+        mine = x if h == 0 else y
+        total = (
+            wide(first_buf, h, z, mine)
+            + wide(core_buf, h, chip_of(z, x, y))
+            + wide(second_buf, h, z)
+        )
+
+        @pl.when(z == 0)
+        def _():
+            arrive(down_buf, down_sem, (h, z), Z_DOWN)
+            out_ref[rows(h)] = (total + wide(down_buf, h, z)).astype(jnp.bfloat16)
+
+        @pl.when(z == NZ - 1)
+        def _():
+            arrive(up_buf, up_sem, (h, z), Z_UP)
+            out_ref[rows(h)] = (total + wide(up_buf, h, z)).astype(jnp.bfloat16)
+
+        @pl.when(jnp.logical_and(z > 0, z < NZ - 1))
+        def _():
+            arrive(down_buf, down_sem, (h, z), Z_DOWN)
+            arrive(up_buf, up_sem, (h, z), Z_UP)
+            both = wide(up_buf, h, z) + wide(down_buf, h, z)
+            out_ref[rows(h)] = (total + both).astype(jnp.bfloat16)
+
+    for wait in sent:
+        wait()
+
+
+def reduce_plots(terms):
+    length = terms.shape[1]
+    half = length // 2
+
+    def blocks(*lead):
+        return pltpu.VMEM((*lead, half, D), jnp.bfloat16)
+
+    return pl.pallas_call(
+        reduce_kernel,
+        out_shape=jax.ShapeDtypeStruct((length, D), jnp.bfloat16),
+        in_specs=[pl.BlockSpec(memory_space=pltpu.VMEM)],
+        out_specs=pl.BlockSpec(memory_space=pltpu.VMEM),
+        scratch_shapes=[
+            blocks(2, CHIPS),
+            blocks(2, NZ, 2),
+            blocks(2, NZ),
+            blocks(2, NZ),
+            blocks(2, NZ),
+            pltpu.SemaphoreType.DMA((2, 2, CHIPS)),
+            pltpu.SemaphoreType.DMA((2, 2, NZ, 2)),
+            pltpu.SemaphoreType.DMA((2, 2, NZ)),
+            pltpu.SemaphoreType.DMA((2, 2, NZ)),
+            pltpu.SemaphoreType.DMA((2, 2, NZ)),
+        ],
+        compiler_params=pltpu.CompilerParams(
+            collective_id=1, has_side_effects=True, vmem_limit_bytes=48 * 1024 * 1024
+        ),
+    )(terms)
+
+
+def slot_positions(crop_ids, capacity):
+    length = crop_ids.shape[0]
+    same = crop_ids[:, None] == crop_ids[None, :]
+    earlier = jnp.arange(length)[None, :] < jnp.arange(length)[:, None]
+    slot_ids = jnp.sum(jnp.logical_and(same, earlier).astype(jnp.int32), axis=1)
+    return crop_ids * capacity + slot_ids
+
+
+def routed_experts(routed, crop_ids, w_gate, w_up, w_down):
+    length = routed.shape[0]
+    capacity = length // 4
+    plots = CHIPS * NC
+    local_count = w_gate.shape[0]
+    position = slot_positions(crop_ids, capacity)
+    everywhere = lax.all_gather(position, ("dp", "expert"), axis=0)
+    tokens = gather_plots(routed)
+    held = local_count * capacity
+    slots = lax.axis_index("expert") * held + jnp.arange(held, dtype=jnp.int32)
+    select = (everywhere[:, None, :] == slots[None, :, None]).astype(jnp.bfloat16)
+    select = select.reshape(plots, local_count, capacity, length)
+    packed = jnp.einsum(
+        "pjct,ptd->jpcd", select, tokens, preferred_element_type=jnp.float32
+    ).astype(jnp.bfloat16)
+    packed = packed.reshape(local_count, plots * capacity, D)
+    gate_act = jnp.einsum("jrd,jdf->jrf", packed, w_gate, preferred_element_type=jnp.float32)
+    up_act = jnp.einsum("jrd,jdf->jrf", packed, w_up, preferred_element_type=jnp.float32)
+    hidden = (jax.nn.silu(gate_act) * up_act).astype(jnp.bfloat16)
+    term = jnp.einsum("jrf,jfd->jrd", hidden, w_down, preferred_element_type=jnp.float32)
+    term = term.astype(jnp.bfloat16).reshape(local_count, plots, capacity, D)
+    by_token = jnp.einsum(
+        "pjct,jpcd->ptd", select, term, preferred_element_type=jnp.float32
+    ).astype(jnp.bfloat16)
+    return reduce_plots(by_token)
 
 
 def rms_scale(values, width_eps):
@@ -101,6 +496,10 @@
         jnp.bfloat16
     )
     crop_ids = crops.reshape(length)
+    if lax.axis_size("dp") == NZ * NX and lax.axis_size("expert") == NY * NC:
+        expert_out = routed_experts(routed, crop_ids, w_gate, w_up, w_down)
+        layer_sum = (resid_wide + expert_out.astype(jnp.float32)).astype(jnp.bfloat16)
+        return layer_sum.reshape(1, 1, length, D)
     onehot = (crop_ids[:, None] == jnp.arange(EXPERTS, dtype=jnp.int32)[None, :]).astype(jnp.int32)
     slot_ids = jnp.sum((jnp.cumsum(onehot, axis=0) - onehot) * onehot, axis=1)
     capacity = length // 4

time: 338 us -> 271 us (0.80)
  waiting for transfers between devices: 217 us -> 0.01 us
  Pallas kernels: 0 us -> 128 us
  matrix products: 47.8 us -> 67 us
  between operations: 13.7 us -> 0.27 us
  blocking collectives: 29.9 us -> 41.7 us
    pallas_call x0 -> x2, Pallas kernels: none -> 128 us  [the longest x1 69.8 us: reduce_plots(): pl.pallas_call(reduce_kernel, out_shape=jax.ShapeDtypeStruct((length, D),...]
    reduce_scatter x1 -> x0, waiting for transfers between devices: 116 us -> none  [on_device(): lax.psum_scatter(term.reshape(1 * lax.axis_size('dp'), owners, local_coun...]
    all_gather x1 -> x0, waiting for transfers between devices: 97.2 us -> none  [spread(): return lax.all_gather(buffers, 'dp', axis=0, tiled=True)]
    all_gather x0 -> x1, blocking collectives: none -> 41.7 us  [routed_experts(): everywhere = lax.all_gather(position, ('dp', 'expert'), axis=0)]
    all_to_all x2 -> x0, blocking collectives: 29.9 us -> none  [the longest x1 15.1 us: on_device(): lax.all_to_all(own_sums, 'expert', split_axis=0, concat_axis=0, tiled=True)]
    dot_general x5 -> x4, matrix products: 23.8 us -> 41.7 us  [the longest x1 17.9 us: routed_experts(): jnp.einsum('jrf,jfd->jrd', hidden, w_down, preferred_element_type=jnp.flo...]
  transfers between devices with their start and end apart: 3 -> 1, of which waited for: 3 -> 0; matrix products, arithmetic and copies ran while one was open for 3% -> 3% of each run, Pallas kernels for 0% -> 0%
where the time goes in v2:
time: 271 us; the launch traced here: 270 us
  Pallas kernels  128 us (47%)
  matrix products  67 us (25%)
  blocking collectives  41.7 us (15%)
  local copies, waits for them, and re-layouts  15 us (6%)
  other arithmetic  10.4 us (4%)
  starting transfers between devices  7.25 us (3%)
    pallas_call x1, Pallas kernels, reduce_plots(): pl.pallas_call(reduce_kernel, out_shape=jax.ShapeDtypeStruct((length, D),...  69.8 us
    pallas_call x1, Pallas kernels, gather_plots(): pl.pallas_call(gather_kernel, out_shape=jax.ShapeDtypeStruct((plots, leng...  58.6 us
    all_gather x1, blocking collectives, routed_experts(): everywhere = lax.all_gather(position, ('dp', 'expert'), axis=0)  41.7 us
    dot_general x1, matrix products, routed_experts(): jnp.einsum('jrf,jfd->jrd', hidden, w_down, preferred_element_type=jnp.flo...  17.9 us
    dot_general x1, matrix products, routed_experts(): jnp.einsum('pjct,jpcd->ptd', select, term, preferred_element_type=jnp.flo...  10.9 us
    all_to_all x1, starting transfers between devices, on_device(): lax.all_to_all(x_spans, 'dp', split_axis=1, concat_axis=0, tiled=True)  7.25 us
    dot_general x1, matrix products, routed_experts(): jnp.einsum('jrd,jdf->jrf', packed, w_gate, preferred_element_type=jnp.flo...  6.89 us
    dot_general x1, matrix products, routed_experts(): jnp.einsum('pjct,ptd->jpcd', select, tokens, preferred_element_type=jnp.f...  6.04 us
  transfers between devices with their start and end apart: 1, of which 0 were waited for; matrix products, arithmetic and copies ran while one was open for 3% of the time, Pallas kernels for 0%

profile of v2, /device:TPU:0, one launch (start us, length us, event | category | flops | bytes accessed | tf_op | source)
XLA Modules:
  0.0 270.3 jit_solution(5167201868627798379)
XLA Ops:
  0.0 7.3 %all-to-all-start = ((bf16[1,8,1,16,1536]{4,3,2,0,1:T(8,128)(2,1)}), bf16[1,8,1,16,1536]{4,3,2,0,1:T(8,128)(2,1)S(1)}, u32[]{:S(2)}, u32[]{:S(2)}) async-start(bf16[1,8,1,16,1536]{4,3,2,0,1:T(8,128)(2,1)} %bitcast.76), calls=%async_computation | async-start | bytes 786432 | tf_op jit(solution)/shard_map/all_to_all | solution.py:475
  8.0 1.3 convert_element_type.87
  9.2 1.3 convert_element_type.92
  10.5 0.8 copy.89
  13.5 0.9 convert_reduce_fusion
  15.1 41.7 %all-gather = s32[32,1,128]{2,1,0:T(1,128)S(1)} all-gather(s32[1,1,128]{2,1,0:T(1,128)S(1)} %fusion.47), channel_id=1, replica_groups=mesh['dp'=8,'expert'=4] {'dp','expert'}, dimensions={0}, use_global_device_ids=true | all-gather | bytes 16896 | tf_op jit(solution)/shard_map/all_gather | solution.py:387
  58.5 3.1 %convolution_convert_fusion.1 = bf16[128,1536]{1,0:T(8,128)(2,1)S(1)} fusion(bf16[128,1536]{1,0:T(8,128)(2,1)S(1)} %fusion.28, bf16[1536,1536]{1,0:T(8,128)(2,1)} %param.20), kind=kOutput, calls=%fused_computation.15 | convolution fusion | flops 604176384 | bytes 5505024 | tf_op jit(solution)/shard_map/dot_general | solution.py:484
  62.6 3.1 %convolution_convert_fusion.2 = bf16[128,1536]{1,0:T(8,128)(2,1)S(1)} fusion(bf16[128,1536]{1,0:T(8,128)(2,1)S(1)} %fusion.28, bf16[1536,1536]{1,0:T(8,128)(2,1)} %param.19), kind=kOutput, calls=%fused_computation.16 | convolution fusion | flops 604176384 | bytes 5505024 | tf_op jit(solution)/shard_map/dot_general | solution.py:483
  65.7 3.1 %convolution_convert_fusion.3 = bf16[128,1536]{1,0:T(8,128)(2,1)S(1)} fusion(bf16[128,1536]{1,0:T(8,128)(2,1)S(1)} %fusion.28, bf16[1536,1536]{1,0:T(8,128)(2,1)} %param.21), kind=kOutput, calls=%fused_computation.17 | convolution fusion | flops 604176384 | bytes 5505024 | tf_op jit(solution)/shard_map/dot_general | solution.py:485
  68.8 1.3 reshape.141
  70.7 0.9 copy-done
  71.5 1.5 fusion.38
  73.0 2.2 fusion.15
  75.2 3.9 %while.13 = (s32[]{:T(128)}, f32[24,64,64]{2,1,0:T(8,128)S(1)}, f32[2,24,64,64]{3,2,1,0:T(8,128)}, f32[2,24]{1,0:T(2,128)}, f32[2,24,64,64]{3,2,1,0:T(8,128)S(1)}, /*index=5*/s32[]{:T(128)}, s32[]{:T(128)}) while((s32[]{:T(128)}, f32[24,64,64]{2,1,0:T(8,128)S(1)}, f32[2,24,64,64]{3,2,1,0:T(8,128)}, f32[2,24]{1,0:T(2,128)}, ...), condition=%wide.region_3.4_spmd.clone, body=%wide.region_2.3_spmd.clone.sunk | while | flops 393219 | bytes 2359692 | solution.py:448
  75.4 0.7 fusion.67
  76.1 1.0 bitcast_dynamic-update-slice_fusion.2
  78.0 1.0 bitcast_dynamic-update-slice_fusion.2
  79.1 3.6 %fusion.18 = f32[2,24,64,64]{3,2,1,0:T(8,128)S(1)} fusion(f32[2,24,64,64]{3,2,1,0:T(8,128)} %fusion.38, f32[2,24,64]{2,1,0:T(8,128)} %copy.72, pred[64,64]{1,0:T(8,128)(4,1)} %iota_compare_fusion.1, bf16[2,64,24,64]{3,2,1,0:T(8,128)(2,1)} %reshape.141), kind=kOutput, calls=%fused_computation.28 | convolution fusion | flops 151584768 | bytes 1982464 | tf_op jit(solution)/shard_map/nhts,nshd->nthd/dot_general | solution.py:436
  82.7 5.1 %multiply_reduce_fusion = (f32[2,64,24]{1,2,0:T(8,128)S(1)}, f32[2,64,24,64]{1,3,2,0:T(8,128)}) fusion(f32[2,24,64,64]{3,2,1,0:T(8,128)S(1)} %fusion.18, f32[2,24,64,64]{3,2,1,0:T(8,128)S(1)} %copy-done.3, f32[2,64,24]{1,2,0:T(8,128)} %copy.79, bf16[2,64,24,64]{3,2,1,0:T(8,128)(2,1)S(1)} %copy-done.1), kind=kOutput, calls=%fused_computation.20 | convolution fusion | flops 151974912 | bytes 2777088 | tf_op jit(solution)/shard_map/nthd,nhde->nthe/dot_general | solution.py:451
  88.3 1.9 copy.81
  90.2 1.3 reshape.144
  91.5 3.5 %multiply_reduce_fusion.1 = (f32[128]{0:T(128)S(1)}, f32[128,1536]{1,0:T(8,128)S(1)}) fusion(bf16[1536,1536]{1,0:T(8,128)(2,1)} %param.23, f32[128,1536]{1,0:T(8,128)} %reshape.144, f32[128,1536]{1,0:T(8,128)S(1)} %copy.83, f32[1536]{0:T(1024)} %convert_element_type.87, bf16[128,1536]{1,0:T(8,128)(2,1)S(1)} %bitcast.70), kind=kOutput, calls=%fused_computation.40 | convolution fusion | flops 605749120 | bytes 7477760 | tf_op jit(solution)/shard_map/dot_general | solution.py:491
  95.0 0.9 multiply_convert_fusion.2.own_ref
  95.9 58.6 %shard_map.127 = bf16[32,128,1536]{2,1,0:T(8,128)(2,1)} custom-call(bf16[128,1536]{1,0:T(8,128)(2,1)} %multiply_convert_fusion.2.own_ref), custom_call_target="tpu_custom_call" | custom-call | tf_op jit(solution)/shard_map/pallas_call | solution.py:167
  154.5 6.0 %convert_bitcast_fusion = bf16[2,32,32,1536]{3,2,0,1:T(8,128)(2,1)S(1)} fusion(bf16[32,128,1536]{2,1,0:T(8,128)(2,1)} %shard_map.127, s32[2,32]{1,0:T(2,128)S(1)} %copy-done.5, s32[32,128]{1,0:T(8,128)S(1)} %bitcast.77), kind=kOutput, calls=%fused_computation.10 | convolution fusion | flops 808714240 | bytes 18891008 | tf_op jit(solution)/shard_map/pjct,ptd->jpcd/dot_general | solution.py:393
  160.6 0.7 copy.84
  161.3 2.7 copy-done.2
  164.0 6.9 %fusion.51 = f32[2,1024,768]{2,1,0:T(8,128)} fusion(bf16[2,1024,1536]{2,1,0:T(8,128)(2,1)S(1)} %bitcast.71, bf16[2,1536,768]{2,1,0:T(8,128)(2,1)S(1)} %bitcast.83), kind=kOutput, calls=%fused_computation.74 | convolution fusion | flops 4831838208 | bytes 17301504 | tf_op jit(solution)/shard_map/jrd,jdf->jrf/dot_general | solution.py:397
  170.9 17.9 %convolution_convert_fusion = bf16[2,1024,1536]{2,1,0:T(8,128)(2,1)} fusion(bf16[2,768,1536]{2,1,0:T(8,128)(2,1)} %param.27, f32[2,1024,768]{2,1,0:T(8,128)} %fusion.51, bf16[2,1024,1536]{2,1,0:T(8,128)(2,1)} %bitcast.72, bf16[2,1536,768]{2,1,0:T(8,128)(2,1)} %param.26), kind=kOutput, calls=%fused_computation.11 | convolution fusion | flops 9676259328 | bytes 28311552 | tf_op jit(solution)/shard_map/jrf,jfd->jrd/dot_general | solution.py:400
  188.8 10.9 %bitcast_convert_fusion.terms_ref = bf16[32,128,1536]{2,1,0:T(8,128)(2,1)} fusion(bf16[2,32,32,1536]{3,2,1,0:T(8,128)(2,1)} %bitcast.73, s32[2,32]{1,0:T(2,128)S(1)} %copy-done.5, s32[32,128]{1,0:T(8,128)S(1)} %bitcast.78), kind=kOutput, calls=%fused_computation.5 | convolution fusion | flops 811859968 | bytes 18891008 | tf_op jit(solution)/shard_map/pjct,jpcd->ptd/dot_general | solution.py:402
  199.7 69.8 %shard_map.128 = bf16[128,1536]{1,0:T(8,128)(2,1)S(1)} custom-call(bf16[32,128,1536]{2,1,0:T(8,128)(2,1)} %bitcast_convert_fusion.terms_ref), custom_call_target="tpu_custom_call" | custom-call | tf_op jit(solution)/shard_map/pallas_call | solution.py:350
  269.5 0.8 fusion.44
  (46 shorter events, 8.0 us)
Async XLA Ops:
  0.0 58.0 %all-to-all-start = ((bf16[1,8,1,16,1536]{4,3,2,0,1:T(8,128)(2,1)}), bf16[1,8,1,16,1536]{4,3,2,0,1:T(8,128)(2,1)S(1)}, u32[]{:S(2)}, u32[]{:S(2)}) async-start(bf16[1,8,1,16,1536]{4,3,2,0,1:T(8,128)(2,1)} %bitcast.76), calls=%async_computation | async-start | bytes 786432 | tf_op jit(solution)/shard_map/all_to_all | solution.py:475
  11.4 46.6 %copy-start.6 = (f32[2,1,24]{2,1,0:T(1,128)}, f32[2,1,24]{2,1,0:T(1,128)S(1)}, u32[]{:S(2)}) copy-start(f32[2,1,24]{2,1,0:T(1,128)S(1)} %slice.4) | copy-start | bytes 580
  70.6 0.9 copy-start
  75.2 7.5 %copy-start.1 = (bf16[2,64,24,64]{3,2,1,0:T(8,128)(2,1)S(1)}, bf16[2,64,24,64]{3,2,1,0:T(8,128)(2,1)}, u32[]{:S(2)}) copy-start(bf16[2,64,24,64]{3,2,1,0:T(8,128)(2,1)} %copy-done) | copy-start | bytes 1179652
  79.1 3.6 %copy-start.3 = (f32[2,24,64,64]{3,2,1,0:T(8,128)S(1)}, f32[2,24,64,64]{3,2,1,0:T(8,128)}, u32[]{:S(2)}) copy-start(f32[2,24,64,64]{3,2,1,0:T(8,128)} %get-tuple-element.32) | copy-start | bytes 2359300
  91.5 3.5 %copy-start.4 = (f32[1536]{0:T(1024)S(1)}, f32[1536]{0:T(1024)}, u32[]{:S(2)}) copy-start(f32[1536]{0:T(1024)} %convert_element_type.92) | copy-start | bytes 18436
  95.9 58.6 %copy-start.5 = (s32[2,32]{1,0:T(2,128)S(1)}, s32[2,32]{1,0:T(2,128)}, u32[]{:S(2)}) copy-start(s32[2,32]{1,0:T(2,128)} %add_add_fusion) | copy-start | bytes 772
  95.9 68.1 %slice-start = ((s8[4718592]{0:T(1024)(128)(4,1)}), s8[524288]{0:T(1024)(128)(4,1)S(1)}, s32[]{:S(2)}) async-start(s8[4718592]{0:T(1024)(128)(4,1)} %bitcast.82), calls=%async_computation.1 | async-start | bytes 1048576
  154.5 9.5 %slice-start.1 = ((s8[4718592]{0:T(1024)(128)(4,1)}), s8[4194304]{0:T(1024)(128)(4,1)S(1)}, s32[]{:S(2)}) async-start(s8[4718592]{0:T(1024)(128)(4,1)} %bitcast.82), calls=%async_computation.2 | async-start | bytes 8388608
  161.3 2.7 copy-start.2

commit v3 on v2

--- a/solution.py
+++ b/solution.py
@@ -9,7 +9,7 @@
 HEADS = 24
 HEAD_DIM = 64
 EXPERTS = 8
-SPAN = 64
+EXTRA = 16
 NZ = 4
 NX = 2
 NY = 2
@@ -76,12 +76,13 @@
 
 def gather_kernel(own_ref, out_ref, send_sem, recv_sem, core_sem, local_sem):
     z, x, y, c = place()
-    half = own_ref.shape[0] // 2
+    length = own_ref.shape[0]
+    half = length // (2 * EXTRA) * EXTRA
     greet(z, x, y, c)
     sent = []
 
     def rows(h):
-        return pl.ds(h * half, half)
+        return pl.ds(h * half, half if h == 0 else length - half)
 
     def copy(h, kind, bz, bx, by, own):
         chip = chip_of(bz, bx, by)
@@ -378,20 +379,18 @@
     return crop_ids * capacity + slot_ids
 
 
-def routed_experts(routed, crop_ids, w_gate, w_up, w_down):
-    length = routed.shape[0]
+def routed_experts(routed, length, w_gate, w_up, w_down):
     capacity = length // 4
     plots = CHIPS * NC
     local_count = w_gate.shape[0]
-    position = slot_positions(crop_ids, capacity)
-    everywhere = lax.all_gather(position, ("dp", "expert"), axis=0)
     tokens = gather_plots(routed)
+    everywhere = tokens[:, length, :length].astype(jnp.int32)
     held = local_count * capacity
     slots = lax.axis_index("expert") * held + jnp.arange(held, dtype=jnp.int32)
     select = (everywhere[:, None, :] == slots[None, :, None]).astype(jnp.bfloat16)
     select = select.reshape(plots, local_count, capacity, length)
     packed = jnp.einsum(
-        "pjct,ptd->jpcd", select, tokens, preferred_element_type=jnp.float32
+        "pjct,ptd->jpcd", jnp.pad(select, ((0, 0),) * 3 + ((0, EXTRA),)), tokens, preferred_element_type=jnp.float32
     ).astype(jnp.bfloat16)
     packed = packed.reshape(local_count, plots * capacity, D)
     gate_act = jnp.einsum("jrd,jdf->jrf", packed, w_gate, preferred_element_type=jnp.float32)
@@ -417,44 +416,146 @@
     return lax.all_to_all(buffers, "expert", split_axis=1, concat_axis=1, tiled=True)
 
 
-def linear_mixing(query, key_vecs, value_vecs, forget, length):
-    blocks = length // SPAN
-    query_narrow = query.reshape(blocks, SPAN, HEADS, HEAD_DIM)
-    key_narrow = key_vecs.reshape(blocks, SPAN, HEADS, HEAD_DIM)
-    query_blocks = query_narrow.astype(jnp.float32)
-    key_blocks = key_narrow.astype(jnp.float32)
-    value_blocks = value_vecs.astype(jnp.float32).reshape(blocks, SPAN, HEADS, HEAD_DIM)
-    within = jnp.cumsum(forget.reshape(blocks, SPAN, HEADS), axis=1)
-    block_total = within[:, -1, :]
-    scores = jnp.einsum(
-        "nthd,nshd->nhts", query_narrow, key_narrow, preferred_element_type=jnp.float32
+def attend_kernel(
+    tokens_ref,
+    column_ref,
+    line_ref,
+    position_ref,
+    attn_gain_ref,
+    query_ref,
+    key_ref,
+    value_ref,
+    head_gain_ref,
+    w_out_ref,
+    moe_gain_ref,
+    resid_ref,
+    routed_ref,
+    normed_ref,
+    total_ref,
+):
+    step = pl.program_id(0)
+    length = tokens_ref.shape[0]
+
+    @pl.when(step == 0)
+    def _():
+        widened = tokens_ref[...].astype(jnp.float32)
+        scaled = widened * rms_scale(widened, 1e-05) * attn_gain_ref[...].astype(jnp.float32)
+        normed_ref[...] = scaled.astype(jnp.bfloat16)
+        total_ref[...] = widened
+
+    def project(ref):
+        return jnp.dot(
+            normed_ref[...], ref[...], preferred_element_type=jnp.float32
+        ).astype(jnp.bfloat16)
+
+    query, key_vecs, value_vecs = project(query_ref), project(key_ref), project(value_ref)
+    lanes = 2 * HEAD_DIM
+    first = lax.broadcasted_iota(jnp.int32, (length, lanes), 1) < HEAD_DIM
+    later = lax.broadcasted_iota(jnp.int32, (length, length), 0)
+    causal = later >= lax.broadcasted_iota(jnp.int32, (length, length), 1)
+    outcome = []
+    for pair in range(query.shape[1] // lanes):
+        cut = slice(pair * lanes, (pair + 1) * lanes)
+        mixed = []
+        for side in range(2):
+            head = 2 * pair + side
+            mask = first if side == 0 else jnp.logical_not(first)
+            chosen = jnp.where(mask, query[:, cut], jnp.zeros((), jnp.bfloat16))
+            scores = lax.dot_general(
+                chosen,
+                key_vecs[:, cut],
+                (((1,), (1,)), ((), ())),
+                preferred_element_type=jnp.float32,
+            )
+            gap = column_ref[0, :, head : head + 1] - line_ref[0, head : head + 1, :]
+            weighted = scores * jnp.exp(jnp.where(causal, gap, -jnp.inf))
+            coarse = weighted.astype(jnp.bfloat16)
+            fine = (weighted - coarse.astype(jnp.float32)).astype(jnp.bfloat16)
+            mixed.append(
+                jnp.dot(coarse, value_vecs[:, cut], preferred_element_type=jnp.float32)
+                + jnp.dot(fine, value_vecs[:, cut], preferred_element_type=jnp.float32)
+            )
+        both = jnp.where(first, mixed[0], mixed[1])
+        square = both * both
+        scale = [
+            lax.rsqrt(
+                jnp.sum(jnp.where(mask, square, 0.0), axis=-1, keepdims=True) / HEAD_DIM + 1e-05
+            )
+            for mask in (first, jnp.logical_not(first))
+        ]
+        gain = head_gain_ref[:, cut].astype(jnp.float32)
+        outcome.append((both * jnp.where(first, scale[0], scale[1]) * gain).astype(jnp.bfloat16))
+    total_ref[...] += jnp.dot(
+        jnp.concatenate(outcome, axis=1), w_out_ref[...], preferred_element_type=jnp.float32
     )
-    by_head = jnp.transpose(within, (0, 2, 1))
-    spread_vals = by_head[:, :, :, None] - by_head[:, :, None, :]
-    causal = jnp.arange(SPAN)[:, None] >= jnp.arange(SPAN)[None, :]
-    weights = jnp.exp(jnp.where(causal[None, None], spread_vals, -jnp.inf))
-    local_part = jnp.einsum(
-        "nhts,nshd->nthd", scores * weights, value_blocks, precision=lax.Precision.HIGHEST
+
+    @pl.when(step == pl.num_programs(0) - 1)
+    def _():
+        resid = total_ref[...].astype(jnp.bfloat16)
+        resid_ref[...] = resid
+        wide = resid.astype(jnp.float32)
+        scaled = wide * rms_scale(wide, 1e-05) * moe_gain_ref[...].astype(jnp.float32)
+        routed_ref[:length, :] = scaled.astype(jnp.bfloat16)
+        extra = routed_ref.shape[0] - length
+        routed_ref[length:, :] = jnp.zeros((extra, D), jnp.bfloat16)
+        routed_ref[length:, :length] = jnp.broadcast_to(
+            position_ref[...].astype(jnp.float32), (extra, length)
+        ).astype(jnp.bfloat16)
+
+
+def attend(
+    tokens, forget, position, attn_gain, w_query, w_key, w_value, head_gain, w_out, moe_gain
+):
+    length = tokens.shape[0]
+    steps = 6
+    width = D // steps
+    cumulative = jnp.cumsum(forget, axis=0)
+    line = cumulative.T.reshape(steps, HEADS // steps, length)
+    column = jnp.transpose(line, (0, 2, 1))
+
+    def whole(*shape):
+        return pl.BlockSpec(shape, lambda j: (0,) * len(shape))
+
+    columns = pl.BlockSpec((D, width), lambda j: (0, j))
+    return pl.pallas_call(
+        attend_kernel,
+        grid=(steps,),
+        out_shape=(
+            jax.ShapeDtypeStruct((length, D), jnp.bfloat16),
+            jax.ShapeDtypeStruct((length + EXTRA, D), jnp.bfloat16),
+        ),
+        in_specs=[
+            whole(length, D),
+            pl.BlockSpec((1, length, HEADS // steps), lambda j: (j, 0, 0)),
+            pl.BlockSpec((1, HEADS // steps, length), lambda j: (j, 0, 0)),
+            whole(1, length),
+            whole(1, D),
+            columns,
+            columns,
+            columns,
+            pl.BlockSpec((1, width), lambda j: (0, j)),
+            pl.BlockSpec((width, D), lambda j: (j, 0)),
+            whole(1, D),
+        ],
+        out_specs=(whole(length, D), whole(length + EXTRA, D)),
+        scratch_shapes=[
+            pltpu.VMEM((length, D), jnp.bfloat16),
+            pltpu.VMEM((length, D), jnp.float32),
+        ],
+        compiler_params=pltpu.CompilerParams(vmem_limit_bytes=32 * 1024 * 1024),
+    )(
+        tokens,
+        column,
+        line,
+        position.reshape(1, length),
+        attn_gain.reshape(1, D),
+        w_query,
+        w_key,
+        w_value,
+        head_gain.reshape(1, D),
+        w_out,
+        moe_gain.reshape(1, D),
     )
-    carried_keys = key_blocks * jnp.exp(block_total[:, None, :] - within)[..., None]
-    block_states = jnp.einsum(
-        "nshd,nshe->nhde", carried_keys, value_blocks, precision=lax.Precision.HIGHEST
-    )
-
-    def advance(carried, element):
-        block_state, total_now = element
-        return (carried * jnp.exp(total_now)[:, None, None] + block_state, carried)
-
-    _, entering = lax.scan(
-        advance, jnp.zeros((HEADS, HEAD_DIM, HEAD_DIM), jnp.float32), (block_states, block_total)
-    )
-    earlier_part = jnp.einsum(
-        "nthd,nhde->nthe",
-        query_blocks * jnp.exp(within)[..., None],
-        entering,
-        precision=lax.Precision.HIGHEST,
-    )
-    return (local_part + earlier_part).reshape(length, HEADS, HEAD_DIM)
 
 
 def on_device(
@@ -476,38 +577,21 @@
     length = arrived.shape[0] * arrived.shape[3]
     tokens = arrived.reshape(length, D)
     forget = decay.reshape(length, HEADS)
-    widened = tokens.astype(jnp.float32)
-    normed = (widened * rms_scale(widened, 1e-05) * attn_gain.astype(jnp.float32)).astype(
-        jnp.bfloat16
-    )
-    query = jnp.dot(normed, w_query, preferred_element_type=jnp.float32).astype(jnp.bfloat16)
-    key_vecs = jnp.dot(normed, w_key, preferred_element_type=jnp.float32).astype(jnp.bfloat16)
-    value_vecs = jnp.dot(normed, w_value, preferred_element_type=jnp.float32).astype(jnp.bfloat16)
-    mixed = linear_mixing(query, key_vecs, value_vecs, forget, length)
-    head_scale = head_gain.astype(jnp.float32).reshape(HEADS, HEAD_DIM)
-    head_normed = (
-        (mixed * rms_scale(mixed, 1e-05) * head_scale).reshape(length, D).astype(jnp.bfloat16)
-    )
-    resid = (widened + jnp.dot(head_normed, w_out, preferred_element_type=jnp.float32)).astype(
-        jnp.bfloat16
+    crop_ids = crops.reshape(length)
+    capacity = length // 4
+    position = slot_positions(crop_ids, capacity)
+    resid, routed = attend(
+        tokens, forget, position, attn_gain, w_query, w_key, w_value, head_gain, w_out, moe_gain
     )
     resid_wide = resid.astype(jnp.float32)
-    routed = (resid_wide * rms_scale(resid_wide, 1e-05) * moe_gain.astype(jnp.float32)).astype(
-        jnp.bfloat16
-    )
-    crop_ids = crops.reshape(length)
     if lax.axis_size("dp") == NZ * NX and lax.axis_size("expert") == NY * NC:
-        expert_out = routed_experts(routed, crop_ids, w_gate, w_up, w_down)
+        expert_out = routed_experts(routed, length, w_gate, w_up, w_down)
         layer_sum = (resid_wide + expert_out.astype(jnp.float32)).astype(jnp.bfloat16)
         return layer_sum.reshape(1, 1, length, D)
-    onehot = (crop_ids[:, None] == jnp.arange(EXPERTS, dtype=jnp.int32)[None, :]).astype(jnp.int32)
-    slot_ids = jnp.sum((jnp.cumsum(onehot, axis=0) - onehot) * onehot, axis=1)
-    capacity = length // 4
-    position = crop_ids * capacity + slot_ids
     select = (jnp.arange(EXPERTS * capacity, dtype=jnp.int32)[:, None] == position[None, :]).astype(
         jnp.bfloat16
     )
-    packed = jnp.dot(select, routed, preferred_element_type=jnp.float32).astype(jnp.bfloat16)
+    packed = jnp.dot(select, routed[:length], preferred_element_type=jnp.float32).astype(jnp.bfloat16)
     owners = lax.axis_size("expert")
     local_count = w_gate.shape[0]
     outgoing = packed.reshape(1, owners, EXPERTS * capacity // owners, D)

time: 271 us -> 227 us (0.84)
  blocking collectives: 41.7 us -> 0 us
  matrix products: 67 us -> 44.2 us
  Pallas kernels: 128 us -> 147 us
  waiting for transfers between devices: 0.01 us -> 6.78 us
  other arithmetic: 10.4 us -> 3.67 us
    all_gather x1 -> x0, blocking collectives: 41.7 us -> none  [routed_experts(): everywhere = lax.all_gather(position, ('dp', 'expert'), axis=0)]
    dot_general x9 -> x1, matrix products: 31.3 us -> 6.14 us  [routed_experts(): jnp.einsum('pjct,ptd->jpcd', jnp.pad(select, ((0, 0),) * 3 + ((0, EXTRA),...]
    pallas_call x0 -> x1, Pallas kernels: none -> 10.2 us  [attend(): pl.pallas_call(attend_kernel, grid=(steps,), out_shape=(jax.ShapeDtypeStr...]
    unnamed x18 -> x12, local copies, waits for them, and re-layouts: 3.55 us -> 12.7 us
    pallas_call x1, Pallas kernels: 58.6 us -> 66.4 us  [gather_plots(): pl.pallas_call(gather_kernel, out_shape=jax.ShapeDtypeStruct((plots, leng...]
    all_to_all x1, waiting for transfers between devices: 0.01 us -> 6.78 us  [on_device(): lax.all_to_all(x_spans, 'dp', split_axis=1, concat_axis=0, tiled=True)]
    convert_element_type x5 -> x0, other arithmetic: 4.33 us -> none  [the longest x1 1.29 us: on_device(): moe_gain.astype(jnp.float32)]
    exp x4 -> x0, local copies, waits for them, and re-layouts: 2.74 us -> none  [the longest x2 1.39 us: advance(): return (carried * jnp.exp(total_now)[:, None, None] + block_state, carried)]
  transfers between devices with their start and end apart: 1 -> 1, of which waited for: 0 -> 1; matrix products, arithmetic and copies ran while one was open for 3% -> 2% of each run, Pallas kernels for 0% -> 0%
where the time goes in v3:
time: 227 us; the launch traced here: 226 us
  Pallas kernels  147 us (65%)
  matrix products  44.2 us (19%)
  local copies, waits for them, and re-layouts  16.6 us (7%)
  starting transfers between devices  7.25 us (3%)
  waiting for transfers between devices  6.78 us (3%)
  other arithmetic  3.67 us (2%)
    pallas_call x1, Pallas kernels, reduce_plots(): pl.pallas_call(reduce_kernel, out_shape=jax.ShapeDtypeStruct((length, D),...  70.9 us
    pallas_call x1, Pallas kernels, gather_plots(): pl.pallas_call(gather_kernel, out_shape=jax.ShapeDtypeStruct((plots, leng...  66.4 us
    dot_general x1, matrix products, routed_experts(): jnp.einsum('jrf,jfd->jrd', hidden, w_down, preferred_element_type=jnp.flo...  17.9 us
    unnamed x12, local copies, waits for them, and re-layouts  12.7 us
    dot_general x1, matrix products, routed_experts(): jnp.einsum('pjct,jpcd->ptd', select, term, preferred_element_type=jnp.flo...  10.9 us
    pallas_call x1, Pallas kernels, attend(): pl.pallas_call(attend_kernel, grid=(steps,), out_shape=(jax.ShapeDtypeStr...  10.2 us
    dot_general x1, matrix products, routed_experts(): jnp.einsum('jrd,jdf->jrf', packed, w_gate, preferred_element_type=jnp.flo...  9.26 us
    all_to_all x1, starting transfers between devices, on_device(): lax.all_to_all(x_spans, 'dp', split_axis=1, concat_axis=0, tiled=True)  7.25 us
  transfers between devices with their start and end apart: 1, of which 1 were waited for; matrix products, arithmetic and copies ran while one was open for 2% of the time, Pallas kernels for 0%

profile of v3, /device:TPU:0, one launch (start us, length us, event | category | flops | bytes accessed | tf_op | source)
XLA Modules:
  0.0 226.1 jit_solution(17815001621853539970)
XLA Ops:
  0.0 7.3 %all-to-all-start = ((bf16[1,8,1,16,1536]{4,3,2,0,1:T(8,128)(2,1)}), bf16[1,8,1,16,1536]{4,3,2,0,1:T(8,128)(2,1)S(1)}, u32[]{:S(2)}, u32[]{:S(2)}) async-start(bf16[1,8,1,16,1536]{4,3,2,0,1:T(8,128)(2,1)} %bitcast.40), calls=%async_computation | async-start | bytes 786432 | tf_op jit(solution)/shard_map/all_to_all | solution.py:576
  7.3 0.7 reshape.66.attn_gain_ref
  7.9 0.7 reshape.67.head_gain_ref
  8.6 0.7 reshape.68.moe_gain_ref
  9.3 0.8 copy.30
  10.1 0.2 reduce_window_sum.11
  10.3 0.1 copy.31
  10.4 0.2 copy.32.column_ref
  10.6 0.9 convert_reduce_fusion
  11.5 0.7 bitcast_add_fusion.position_ref
  12.2 6.8 %all-to-all-done = bf16[1,8,1,16,1536]{4,3,2,0,1:T(8,128)(2,1)S(1)} async-done(((bf16[1,8,1,16,1536]{4,3,2,0,1:T(8,128)(2,1)}), bf16[1,8,1,16,1536]{4,3,2,0,1:T(8,128)(2,1)S(1)}, u32[]{:S(2)}, u32[]{:S(2)}) %all-to-all-start) | async-done | bytes 393248 | tf_op jit(solution)/shard_map/all_to_all | solution.py:576
  18.9 0.0 copy-start
  18.9 2.3 %copy-done = bf16[1536,1536]{1,0:T(8,128)(2,1)S(1)} copy-done((bf16[1536,1536]{1,0:T(8,128)(2,1)S(1)}, bf16[1536,1536]{1,0:T(8,128)(2,1)}, u32[]{:S(2)}) %copy-start) | copy-done | bytes 4718616
  21.3 2.3 %copy-done.1 = bf16[1536,1536]{1,0:T(8,128)(2,1)S(1)} copy-done((bf16[1536,1536]{1,0:T(8,128)(2,1)S(1)}, bf16[1536,1536]{1,0:T(8,128)(2,1)}, u32[]{:S(2)}) %copy-start.1) | copy-done | bytes 4718616
  23.6 0.0 copy-start.2
  23.6 2.3 %copy-done.2 = bf16[1536,1536]{1,0:T(8,128)(2,1)S(1)} copy-done((bf16[1536,1536]{1,0:T(8,128)(2,1)S(1)}, bf16[1536,1536]{1,0:T(8,128)(2,1)}, u32[]{:S(2)}) %copy-start.2) | copy-done | bytes 4718616
  26.0 2.3 %copy-done.3 = bf16[1536,1536]{1,0:T(8,128)(2,1)S(1)} copy-done((bf16[1536,1536]{1,0:T(8,128)(2,1)S(1)}, bf16[1536,1536]{1,0:T(8,128)(2,1)}, u32[]{:S(2)}) %copy-start.3) | copy-done | bytes 4718616
  28.3 10.2 %shard_map.127 = (bf16[128,1536]{1,0:T(8,128)(2,1)S(1)}, bf16[144,1536]{1,0:T(8,128)(2,1)S(1)}) custom-call(bf16[128,1536]{1,0:T(8,128)(2,1)S(1)} %bitcast.34, f32[6,128,4]{2,1,0:T(8,128)S(1)} %copy.32.column_ref, f32[6,4,128]{2,1,0:T(4,128)S(1)} %bitcast.36, s32[1,128]{1,0:T(1,128)S(1)} %bitcast_add_fusion.position_ref, ...), custom_call_target="tpu_custom_call" | custom-call | tf_op jit(solution)/shard_map/pallas_call | solution.py:520
  38.5 0.0 copy-start.4
  38.5 0.7 copy-done.4
  39.3 66.4 %shard_map.128 = bf16[32,144,1536]{2,1,0:T(8,128)(2,1)} custom-call(bf16[144,1536]{1,0:T(8,128)(2,1)} %copy-done.4), custom_call_target="tpu_custom_call" | custom-call | tf_op jit(solution)/shard_map/pallas_call | solution.py:168
  105.7 0.9 slice_convert_fusion
  106.5 0.2 broadcast_compare_fusion
  106.8 6.1 %convert_bitcast_fusion = bf16[2,32,32,1536]{3,2,0,1:T(8,128)(2,1)S(1)} fusion(bf16[32,144,1536]{2,1,0:T(8,128)(2,1)} %shard_map.128, pred[32,2,32,128]{3,2,1,0:T(32,128)(4,1)S(1)} %broadcast_compare_fusion), kind=kOutput, calls=%fused_computation.5 | convolution fusion | flops 909115392 | bytes 20709376 | tf_op jit(solution)/shard_map/pjct,ptd->jpcd/dot_general | solution.py:392
  112.9 0.7 copy.33
  113.7 0.0 copy-start.5
  113.7 2.6 %copy-done.5 = bf16[2,32,32,1536]{3,2,1,0:T(8,128)(2,1)} copy-done((bf16[2,32,32,1536]{3,2,1,0:T(8,128)(2,1)}, bf16[2,32,32,1536]{3,2,1,0:T(8,128)(2,1)S(1)}, u32[]{:S(2)}) %copy-start.5) | copy-done | bytes 6291480
  116.3 9.3 %fusion.13 = f32[2,1024,768]{2,1,0:T(8,128)} fusion(bf16[2,1024,1536]{2,1,0:T(8,128)(2,1)S(1)} %bitcast.37, bf16[2,1536,768]{2,1,0:T(8,128)(2,1)} %param.23), kind=kOutput, calls=%fused_computation.21 | convolution fusion | flops 4831838208 | bytes 17301504 | tf_op jit(solution)/shard_map/jrd,jdf->jrf/dot_general | solution.py:396
  125.6 17.9 %convolution_convert_fusion = bf16[2,1024,1536]{2,1,0:T(8,128)(2,1)} fusion(bf16[2,768,1536]{2,1,0:T(8,128)(2,1)} %param.25, f32[2,1024,768]{2,1,0:T(8,128)} %fusion.13, bf16[2,1024,1536]{2,1,0:T(8,128)(2,1)} %bitcast.38, bf16[2,1536,768]{2,1,0:T(8,128)(2,1)} %param.24), kind=kOutput, calls=%fused_computation.6 | convolution fusion | flops 9676259328 | bytes 28311552 | tf_op jit(solution)/shard_map/jrf,jfd->jrd/dot_general | solution.py:399
  143.5 10.9 %bitcast_convert_fusion.terms_ref = bf16[32,128,1536]{2,1,0:T(8,128)(2,1)} fusion(bf16[2,32,32,1536]{3,2,1,0:T(8,128)(2,1)} %bitcast.39, s32[2,32]{1,0:T(2,128)S(1)} %add_add_fusion, s32[32,128]{1,0:T(8,128)S(1)} %bitcast.43), kind=kOutput, calls=%fused_computation | convolution fusion | flops 811859968 | bytes 18891008 | tf_op jit(solution)/shard_map/pjct,jpcd->ptd/dot_general | solution.py:401
  154.4 70.9 %shard_map.129 = bf16[128,1536]{1,0:T(8,128)(2,1)S(1)} custom-call(bf16[32,128,1536]{2,1,0:T(8,128)(2,1)} %bitcast_convert_fusion.terms_ref), custom_call_target="tpu_custom_call" | custom-call | tf_op jit(solution)/shard_map/pallas_call | solution.py:351
  225.3 0.9 fusion.9
  (3 shorter events, 0.0 us)
Async XLA Ops:
  0.0 18.9 %all-to-all-start = ((bf16[1,8,1,16,1536]{4,3,2,0,1:T(8,128)(2,1)}), bf16[1,8,1,16,1536]{4,3,2,0,1:T(8,128)(2,1)S(1)}, u32[]{:S(2)}, u32[]{:S(2)}) async-start(bf16[1,8,1,16,1536]{4,3,2,0,1:T(8,128)(2,1)} %bitcast.40), calls=%async_computation | async-start | bytes 786432 | tf_op jit(solution)/shard_map/all_to_all | solution.py:576
  18.9 2.3 %copy-start = (bf16[1536,1536]{1,0:T(8,128)(2,1)S(1)}, bf16[1536,1536]{1,0:T(8,128)(2,1)}, u32[]{:S(2)}) copy-start(bf16[1536,1536]{1,0:T(8,128)(2,1)} %query_ref.1) | copy-start | bytes 14155780
  21.3 2.3 %copy-start.1 = (bf16[1536,1536]{1,0:T(8,128)(2,1)S(1)}, bf16[1536,1536]{1,0:T(8,128)(2,1)}, u32[]{:S(2)}) copy-start(bf16[1536,1536]{1,0:T(8,128)(2,1)} %key_ref.1) | copy-start | bytes 14155780
  23.6 2.3 %copy-start.2 = (bf16[1536,1536]{1,0:T(8,128)(2,1)S(1)}, bf16[1536,1536]{1,0:T(8,128)(2,1)}, u32[]{:S(2)}) copy-start(bf16[1536,1536]{1,0:T(8,128)(2,1)} %value_ref.1) | copy-start | bytes 14155780
  26.0 2.3 %copy-start.3 = (bf16[1536,1536]{1,0:T(8,128)(2,1)S(1)}, bf16[1536,1536]{1,0:T(8,128)(2,1)}, u32[]{:S(2)}) copy-start(bf16[1536,1536]{1,0:T(8,128)(2,1)} %w_out_ref.1) | copy-start | bytes 14155780
  38.5 0.8 copy-start.4
  113.7 2.7 %copy-start.5 = (bf16[2,32,32,1536]{3,2,1,0:T(8,128)(2,1)}, bf16[2,32,32,1536]{3,2,1,0:T(8,128)(2,1)S(1)}, u32[]{:S(2)}) copy-start(bf16[2,32,32,1536]{3,2,1,0:T(8,128)(2,1)S(1)} %copy.33) | copy-start | bytes 18874372

commit v4 on v3

--- a/solution.py
+++ b/solution.py
@@ -379,28 +379,73 @@
     return crop_ids * capacity + slot_ids
 
 
+def experts_kernel(
+    base_ref, tokens_ref, w_gate_ref, w_up_ref, w_down_ref, out_ref, packed_ref, term_ref
+):
+    plots, length = out_ref.shape[0], out_ref.shape[1]
+    experts = w_gate_ref.shape[0]
+    capacity = packed_ref.shape[1] // plots
+    held = experts * capacity
+    slots = lax.broadcasted_iota(jnp.int32, (held, length), 0) + base_ref[0]
+
+    def select(plot):
+        position = tokens_ref[plot, length:, :length].astype(jnp.float32)[:1]
+        hit = slots == position.astype(jnp.int32)
+        return jnp.where(hit, 1.0, 0.0).astype(jnp.bfloat16)
+
+    for plot in range(plots):
+        rows = jnp.dot(
+            select(plot), tokens_ref[plot, :length, :], preferred_element_type=jnp.float32
+        ).astype(jnp.bfloat16)
+        for j in range(experts):
+            packed_ref[j, plot * capacity : (plot + 1) * capacity, :] = rows[
+                j * capacity : (j + 1) * capacity
+            ]
+    for j in range(experts):
+        packed = packed_ref[j]
+        gate_act = jnp.dot(packed, w_gate_ref[j], preferred_element_type=jnp.float32)
+        up_act = jnp.dot(packed, w_up_ref[j], preferred_element_type=jnp.float32)
+        hidden = (gate_act / (1.0 + jnp.exp(-gate_act)) * up_act).astype(jnp.bfloat16)
+        term_ref[j] = jnp.dot(
+            hidden, w_down_ref[j], preferred_element_type=jnp.float32
+        ).astype(jnp.bfloat16)
+    for plot in range(plots):
+        cut = slice(plot * capacity, (plot + 1) * capacity)
+        term = jnp.concatenate([term_ref[j, cut, :] for j in range(experts)], axis=0)
+        out_ref[plot] = lax.dot_general(
+            select(plot), term, (((0,), (0,)), ((), ())), preferred_element_type=jnp.float32
+        ).astype(jnp.bfloat16)
+
+
 def routed_experts(routed, length, w_gate, w_up, w_down):
     capacity = length // 4
     plots = CHIPS * NC
-    local_count = w_gate.shape[0]
+    group = plots // NZ
+    local_count, _, width = w_gate.shape
     tokens = gather_plots(routed)
-    everywhere = tokens[:, length, :length].astype(jnp.int32)
-    held = local_count * capacity
-    slots = lax.axis_index("expert") * held + jnp.arange(held, dtype=jnp.int32)
-    select = (everywhere[:, None, :] == slots[None, :, None]).astype(jnp.bfloat16)
-    select = select.reshape(plots, local_count, capacity, length)
-    packed = jnp.einsum(
-        "pjct,ptd->jpcd", jnp.pad(select, ((0, 0),) * 3 + ((0, EXTRA),)), tokens, preferred_element_type=jnp.float32
-    ).astype(jnp.bfloat16)
-    packed = packed.reshape(local_count, plots * capacity, D)
-    gate_act = jnp.einsum("jrd,jdf->jrf", packed, w_gate, preferred_element_type=jnp.float32)
-    up_act = jnp.einsum("jrd,jdf->jrf", packed, w_up, preferred_element_type=jnp.float32)
-    hidden = (jax.nn.silu(gate_act) * up_act).astype(jnp.bfloat16)
-    term = jnp.einsum("jrf,jfd->jrd", hidden, w_down, preferred_element_type=jnp.float32)
-    term = term.astype(jnp.bfloat16).reshape(local_count, plots, capacity, D)
-    by_token = jnp.einsum(
-        "pjct,jpcd->ptd", select, term, preferred_element_type=jnp.float32
-    ).astype(jnp.bfloat16)
+    base = (lax.axis_index("expert") * (local_count * capacity)).astype(jnp.int32).reshape(1)
+
+    def resident(*shape):
+        return pl.BlockSpec(shape, lambda i: (0, 0, 0), pipeline_mode=pl.Buffered(1))
+
+    by_token = pl.pallas_call(
+        experts_kernel,
+        grid=(NZ,),
+        out_shape=jax.ShapeDtypeStruct((plots, length, D), jnp.bfloat16),
+        in_specs=[
+            pl.BlockSpec(memory_space=pltpu.SMEM),
+            pl.BlockSpec((group, length + EXTRA, D), lambda i: (i, 0, 0)),
+            resident(local_count, D, width),
+            resident(local_count, D, width),
+            resident(local_count, width, D),
+        ],
+        out_specs=pl.BlockSpec((group, length, D), lambda i: (i, 0, 0)),
+        scratch_shapes=[
+            pltpu.VMEM((local_count, group * capacity, D), jnp.bfloat16),
+            pltpu.VMEM((local_count, group * capacity, D), jnp.bfloat16),
+        ],
+        compiler_params=pltpu.CompilerParams(vmem_limit_bytes=56 * 1024 * 1024),
+    )(base, tokens, w_gate, w_up, w_down)
     return reduce_plots(by_token)
 
 
@@ -542,7 +587,7 @@
             pltpu.VMEM((length, D), jnp.bfloat16),
             pltpu.VMEM((length, D), jnp.float32),
         ],
-        compiler_params=pltpu.CompilerParams(vmem_limit_bytes=32 * 1024 * 1024),
+        compiler_params=pltpu.CompilerParams(vmem_limit_bytes=56 * 1024 * 1024),
     )(
         tokens,
         column,

time: 227 us -> 200 us (0.88)
  matrix products: 44.2 us -> 0 us
  Pallas kernels: 147 us -> 179 us
  local copies, waits for them, and re-layouts: 16.6 us -> 6.42 us
  waiting for transfers between devices: 6.78 us -> 3.75 us
    dot_general x4 -> x0, matrix products: 44.2 us -> none  [the longest x1 17.9 us: routed_experts(): jnp.einsum('jrf,jfd->jrd', hidden, w_down, preferred_element_type=jnp.flo...]
    pallas_call x0 -> x1, Pallas kernels: none -> 28.3 us  [routed_experts(): pl.pallas_call(experts_kernel, grid=(NZ,), out_shape=jax.ShapeDtypeStruct...]
    unnamed x12 -> x6, local copies, waits for them, and re-layouts: 12.7 us -> 0.75 us
    pallas_call x1, Pallas kernels: 10.2 us -> 13.5 us  [attend(): pl.pallas_call(attend_kernel, grid=(steps,), out_shape=(jax.ShapeDtypeStr...]
    all_to_all x1, waiting for transfers between devices: 6.78 us -> 3.75 us  [on_device(): lax.all_to_all(x_spans, 'dp', split_axis=1, concat_axis=0, tiled=True)]
  transfers between devices with their start and end apart: 1 -> 1, of which waited for: 1 -> 1; matrix products, arithmetic and copies ran while one was open for 2% -> 4% of each run, Pallas kernels for 0% -> 0%
where the time goes in v4:
time: 200 us
  Pallas kernels  179 us (90%)
  starting transfers between devices  7.25 us (4%)
  local copies, waits for them, and re-layouts  6.42 us (3%)
  waiting for transfers between devices  3.75 us (2%)
  other arithmetic  3.09 us (2%)
    pallas_call x1, Pallas kernels, reduce_plots(): pl.pallas_call(reduce_kernel, out_shape=jax.ShapeDtypeStruct((length, D),...  70.9 us
    pallas_call x1, Pallas kernels, gather_plots(): pl.pallas_call(gather_kernel, out_shape=jax.ShapeDtypeStruct((plots, leng...  66.4 us
    pallas_call x1, Pallas kernels, routed_experts(): pl.pallas_call(experts_kernel, grid=(NZ,), out_shape=jax.ShapeDtypeStruct...  28.3 us
    pallas_call x1, Pallas kernels, attend(): pl.pallas_call(attend_kernel, grid=(steps,), out_shape=(jax.ShapeDtypeStr...  13.5 us
    all_to_all x1, starting transfers between devices, on_device(): lax.all_to_all(x_spans, 'dp', split_axis=1, concat_axis=0, tiled=True)  7.25 us
  transfers between devices with their start and end apart: 1, of which 1 were waited for; matrix products, arithmetic and copies ran while one was open for 4% of the time, Pallas kernels for 0%

profile of v4, /device:TPU:0, one launch (start us, length us, event | category | flops | bytes accessed | tf_op | source)
XLA Modules:
  0.0 199.6 jit_solution(2234068464188654390)
XLA Ops:
  0.0 7.3 %all-to-all-start = ((bf16[1,8,1,16,1536]{4,3,2,0,1:T(8,128)(2,1)}), bf16[1,8,1,16,1536]{4,3,2,0,1:T(8,128)(2,1)S(1)}, u32[]{:S(2)}, u32[]{:S(2)}) async-start(bf16[1,8,1,16,1536]{4,3,2,0,1:T(8,128)(2,1)} %bitcast.16), calls=%async_computation | async-start | bytes 786432 | tf_op jit(solution)/shard_map/all_to_all | solution.py:621
  7.3 1.3 reshape.54.attn_gain_ref
  8.5 1.3 reshape.55.head_gain_ref
  9.8 1.3 reshape.56.moe_gain_ref
  11.1 0.8 copy.22
  11.9 0.2 reduce_window_sum.11
  12.1 0.1 copy.23
  12.1 0.0 copy-start.2
  12.1 1.0 copy.24.column_ref
  13.1 0.9 convert_reduce_fusion
  14.0 1.2 bitcast_add_fusion.position_ref
  15.2 3.7 %all-to-all-done = bf16[1,8,1,16,1536]{4,3,2,0,1:T(8,128)(2,1)S(1)} async-done(((bf16[1,8,1,16,1536]{4,3,2,0,1:T(8,128)(2,1)}), bf16[1,8,1,16,1536]{4,3,2,0,1:T(8,128)(2,1)S(1)}, u32[]{:S(2)}, u32[]{:S(2)}) %all-to-all-start) | async-done | bytes 393248 | tf_op jit(solution)/shard_map/all_to_all | solution.py:621
  18.9 0.0 copy-start
  18.9 0.0 copy-done.2
  19.0 0.7 copy-done
  19.7 13.5 %shard_map.127 = (bf16[128,1536]{1,0:T(8,128)(2,1)}, bf16[144,1536]{1,0:T(8,128)(2,1)}) custom-call(bf16[128,1536]{1,0:T(8,128)(2,1)} %bitcast.15, f32[6,128,4]{2,1,0:T(8,128)} %copy.24.column_ref, f32[6,4,128]{2,1,0:T(4,128)} %bitcast.19, s32[1,128]{1,0:T(1,128)} %bitcast_add_fusion.position_ref, bf16[1,1536]{1,0:T(2,128)(2,1)} %reshape.54.attn_gain_ref, ...), custom_call_target="tpu_custom_call" | custom-call | tf_op jit(solution)/shard_map/pallas_call | solution.py:565
  33.2 66.4 %shard_map.128.tokens_ref = bf16[32,144,1536]{2,1,0:T(8,128)(2,1)} custom-call(bf16[144,1536]{1,0:T(8,128)(2,1)} %get-tuple-element.8.own_ref), custom_call_target="tpu_custom_call" | custom-call | tf_op jit(solution)/shard_map/pallas_call | solution.py:168
  99.6 28.3 %shard_map.129.terms_ref = bf16[32,128,1536]{2,1,0:T(8,128)(2,1)} custom-call(s32[1]{0:T(128)} %bitcast.9.base_ref, bf16[32,144,1536]{2,1,0:T(8,128)(2,1)} %shard_map.128.tokens_ref, bf16[2,1536,768]{2,1,0:T(8,128)(2,1)} %w_gate_ref.1, bf16[2,1536,768]{2,1,0:T(8,128)(2,1)} %w_up_ref.1, bf16[2,768,1536]{2,1,0:T(8,128)(2,1)} %w_down_ref.1), custom_call_target="tpu_custom_call" | custom-call | tf_op jit(solution)/shard_map/pallas_call | solution.py:431
  127.9 0.0 copy-start.1
  127.9 70.9 %shard_map.130 = bf16[128,1536]{1,0:T(8,128)(2,1)S(1)} custom-call(bf16[32,128,1536]{2,1,0:T(8,128)(2,1)} %shard_map.129.terms_ref), custom_call_target="tpu_custom_call" | custom-call | tf_op jit(solution)/shard_map/pallas_call | solution.py:351
  198.8 0.0 copy-done.1
  198.8 0.8 fusion
Async XLA Ops:
  0.0 18.9 %all-to-all-start = ((bf16[1,8,1,16,1536]{4,3,2,0,1:T(8,128)(2,1)}), bf16[1,8,1,16,1536]{4,3,2,0,1:T(8,128)(2,1)S(1)}, u32[]{:S(2)}, u32[]{:S(2)}) async-start(bf16[1,8,1,16,1536]{4,3,2,0,1:T(8,128)(2,1)} %bitcast.16), calls=%async_computation | async-start | bytes 786432 | tf_op jit(solution)/shard_map/all_to_all | solution.py:621
  12.1 6.8 %copy-start.2 = (f32[24,128]{1,0:T(8,128)}, f32[24,128]{1,0:T(8,128)S(1)}, u32[]{:S(2)}) copy-start(f32[24,128]{1,0:T(8,128)S(1)} %copy.23) | copy-start | bytes 36868
  18.9 0.7 copy-start
  127.9 70.9 %copy-start.1 = (bf16[128,1536]{1,0:T(8,128)(2,1)S(1)}, bf16[128,1536]{1,0:T(8,128)(2,1)}, u32[]{:S(2)}) copy-start(bf16[128,1536]{1,0:T(8,128)(2,1)} %get-tuple-element.7) | copy-start | bytes 1179652
